TPU v7x, 32 devices: a whole 2x2x4 slice. The times are simulated.
32 devices in a mesh: seq: 8 (over y, x, core), wsh: 4 (over z).
Axes of the slice: x: 2, y: 2, z: 4, core: 2. Of those that a mesh axis runs over, the one named last changes fastest.
Arguments:
- x_in: bfloat16 [4, 4096, 1024], P('wsh', 'seq'), may hold values from -6 to 6
- seg_ids: int32 [4, 4096], P('wsh', 'seq'), may hold values from 0 to 7, never falling along the last dimension, each value on 1 to 2048 neighbouring positions
- in_weight: bfloat16 [1024, 4384], P('wsh'), may hold values from -0.1875 to 0.1875
- out_weight: bfloat16 [2048, 1024], P('wsh'), may hold values from -0.125 to 0.125
- conv_weight: bfloat16 [4, 2304], P(None, 'wsh'), may hold values from -3 to 3
- conv_bias: bfloat16 [2304], P('wsh'), may hold values from -0.5 to 0.5
- dt_bias: bfloat16 [32], P('wsh'), may hold values from -6 to -3
- a_log: bfloat16 [32], P('wsh'), may hold values from -4 to 1.5
- skip_gain: bfloat16 [32], P('wsh'), may hold values from 0.5 to 1.5
- norm_gain: bfloat16 [1024], P('wsh'), may hold values from 0.5 to 1.5
- gate_gain: bfloat16 [2048], P('wsh'), may hold values from 0.5 to 1.5
- cotangent: bfloat16 [4, 4096, 1024], P('wsh', 'seq'), may hold values from -6 to 6
Outputs:
- output: bfloat16 [4, 4096, 1024], P('wsh', 'seq')
- grad_input: float32 [4, 4096, 1024], P('wsh', 'seq')
- grad_in_weight: float32 [1024, 4384], P('wsh')
- grad_out_weight: float32 [2048, 1024], P('wsh')
- grad_conv_weight: float32 [4, 2304], P(None, 'wsh')
- grad_conv_bias: float32 [2304], P('wsh')
- grad_dt_bias: float32 [32], P('wsh')
- grad_a_log: float32 [32], P('wsh')
- grad_skip: float32 [32], P('wsh')
- grad_norm_gain: float32 [1024], P('wsh')
- grad_gate_gain: float32 [2048], P('wsh')
Inputs may be any that keep to these rules, and one draw needn't show every extreme that they name: `seg_ids`: in each stream, document numbers never fall, each document has 1 to 2048 rows and one has exactly 2048.
All inputs are finite; a program needn't handle non-finite values.
Results may differ from a plain program's by a relative error of at most 0.012.
The roundings to bfloat16 on the way count: a program that leaves them out, or rounds other values in their place, can miss the bound.
Values may be sent and summed in bfloat16 or wider, within the bound.
No kernel may reach another device: no remote copies, remote signals or barrier semaphores. Data moves between devices by JAX's collectives and lax.ppermute only.
A program may use at most 192 MiB of HBM per device.

v0:
```python
import jax
import jax.numpy as jnp
from jax import lax
from jax.sharding import PartitionSpec as P

BLOCK = 512


epsilon = 1e-05
highest = lax.Precision.HIGHEST


def shifted(value, axis, steps):
    count = lax.axis_size(axis)
    first, last = (max(0, -steps), min(count, count - steps))
    return lax.ppermute(value, axis, [(source, source + steps) for source in range(first, last)])


def rms_scale(values, gain_vec):
    return (
        values * lax.rsqrt(jnp.mean(values * values, axis=-1, keepdims=True) + epsilon) * gain_vec
    )


def gated_norm(scanned, gate_part, gain_vec):
    return rms_scale(scanned * jax.nn.silu(gate_part), gain_vec)


def conv_silu(extended, ext_ids, conv_weight, conv_bias):
    tap_count = conv_weight.shape[0]
    rows_count = extended.shape[0] - tap_count + 1
    current = ext_ids[tap_count - 1 :]
    summed = jnp.zeros((rows_count, extended.shape[1]), jnp.float32) + conv_bias[None, :]
    for offset in range(tap_count):
        window = extended[offset : offset + rows_count]
        matching = (ext_ids[offset : offset + rows_count] == current).astype(jnp.float32)
        summed = summed + window * conv_weight[offset][None, :] * matching[:, None]
    return jax.nn.silu(summed)


def scan_heads(head_x, head_dt, b_rows, c_rows, segment_ids, dt_bias, a_log, skip_gain, block_rows):
    length = head_x.shape[0]
    head_count = head_dt.shape[1]
    head_dim = head_x.shape[1] // head_count
    state_dim = b_rows.shape[1]
    blocks = length // block_rows
    step_size = jax.nn.softplus(head_dt + dt_bias[None, :])
    log_decay = -jnp.exp(a_log)[None, :] * step_size
    x_heads = head_x.reshape(length, head_count, head_dim)
    scaled = x_heads * step_size[:, :, None]
    prev_ids = jnp.concatenate(
        [jnp.full((1,), -1, jnp.int32), segment_ids[block_rows - 1 :: block_rows][:-1]]
    )
    lower_mask = jnp.tril(jnp.ones((block_rows, block_rows), jnp.bool_))

    def one_block(carry_state, pieces):
        decay_part, scaled_part, b_part, c_part, id_part, prev_id = pieces
        cumulative = jnp.cumsum(decay_part, axis=0)
        linked = (id_part[:, None] == id_part[None, :]) & lower_mask
        differ = cumulative.T[:, :, None] - cumulative.T[:, None, :]
        kernel = jnp.where(linked[None], jnp.exp(jnp.where(linked[None], differ, 0.0)), 0.0)
        scores = jnp.dot(c_part, b_part.T, precision=highest)
        mixed_kernel = kernel * scores[None]
        intra_out = jnp.einsum("hts,shp->thp", mixed_kernel, scaled_part, precision=highest)
        carried = (id_part == prev_id).astype(jnp.float32)
        carry_in = jnp.exp(cumulative) * carried[:, None]
        inter_out = (
            jnp.einsum("tn,hpn->thp", c_part, carry_state, precision=highest) * carry_in[:, :, None]
        )
        end_link = (id_part == id_part[-1]).astype(jnp.float32)
        to_end = jnp.exp(cumulative[-1][None, :] - cumulative) * end_link[:, None]
        fresh = jnp.einsum(
            "shp,sn->hpn", to_end[:, :, None] * scaled_part, b_part, precision=highest
        )
        block_decay = jnp.exp(cumulative[-1]) * carried[-1]
        new_state = carry_state * block_decay[:, None, None] + fresh
        return (new_state, intra_out + inter_out)

    pieces = (
        log_decay.reshape(blocks, block_rows, head_count),
        scaled.reshape(blocks, block_rows, head_count, head_dim),
        b_rows.reshape(blocks, block_rows, state_dim),
        c_rows.reshape(blocks, block_rows, state_dim),
        segment_ids.reshape(blocks, block_rows),
        prev_ids,
    )
    initial = jnp.zeros((head_count, head_dim, state_dim), jnp.float32)
    ignored, outputs = lax.scan(jax.checkpoint(one_block), initial, pieces)
    result = outputs.reshape(length, head_count, head_dim) + skip_gain[None, :, None] * x_heads
    return result.reshape(length, head_count * head_dim)


def local(
    x_in,
    seg_ids,
    in_weight,
    out_weight,
    conv_weight,
    conv_bias,
    dt_bias,
    a_log,
    skip_gain,
    norm_gain,
    gate_gain,
    cotangent,
):
    w_in, w_out, conv_full, bias_full, dt_full, alog_full, skip_full, norm_full, gate_full = (
        lax.all_gather(in_weight, "wsh", axis=0, tiled=True),
        lax.all_gather(out_weight, "wsh", axis=0, tiled=True),
        lax.all_gather(conv_weight, "wsh", axis=1, tiled=True),
        lax.all_gather(conv_bias, "wsh", axis=0, tiled=True),
        lax.all_gather(dt_bias, "wsh", axis=0, tiled=True),
        lax.all_gather(a_log, "wsh", axis=0, tiled=True),
        lax.all_gather(skip_gain, "wsh", axis=0, tiled=True),
        lax.all_gather(norm_gain, "wsh", axis=0, tiled=True),
        lax.all_gather(gate_gain, "wsh", axis=0, tiled=True),
    )
    tok_rows = x_in.shape[1]
    seq_count = lax.axis_size("seq")
    seq_index = lax.axis_index("seq")
    row_start = seq_index * tok_rows
    inner_width = w_out.shape[0]
    head_count = dt_full.shape[0]
    state_dim = (w_in.shape[1] - 2 * inner_width - head_count) // 2
    channels = inner_width + 2 * state_dim
    tap_count = conv_full.shape[0]
    residual_in = x_in[0].astype(jnp.float32)
    ids_full = lax.all_gather(seg_ids, "seq", axis=1, tiled=True)[0]
    normed_f, norm_pull = jax.vjp(rms_scale, residual_in, norm_full.astype(jnp.float32))
    normed = normed_f.astype(jnp.bfloat16)
    projected = jnp.dot(normed, w_in, preferred_element_type=jnp.float32).astype(jnp.bfloat16)
    gate_part = projected[:, :inner_width]
    conv_in = projected[:, inner_width : inner_width + channels]
    dt_part = projected[:, inner_width + channels :]
    halo_rows = shifted(conv_in[tok_rows - (tap_count - 1) :], "seq", 1)
    extended = jnp.concatenate([halo_rows, conv_in]).astype(jnp.float32)
    padded_ids = jnp.concatenate([jnp.full((tap_count - 1,), -1, jnp.int32), ids_full])
    ext_ids = lax.dynamic_slice_in_dim(padded_ids, row_start, tok_rows + tap_count - 1)

    def conv_local(ext_rows, weights, biases):
        return conv_silu(ext_rows, ext_ids, weights, biases)

    activated, conv_pull = jax.vjp(
        conv_local, extended, conv_full.astype(jnp.float32), bias_full.astype(jnp.float32)
    )
    x_part = activated[:, :inner_width].astype(jnp.bfloat16)
    bc_part = activated[:, inner_width:].astype(jnp.bfloat16)
    head_x, head_dt = (
        lax.all_to_all(x_part, "seq", split_axis=1, concat_axis=0, tiled=True),
        lax.all_to_all(dt_part, "seq", split_axis=1, concat_axis=0, tiled=True),
    )
    bc_full = lax.all_gather(bc_part, "seq", axis=0, tiled=True)
    local_heads = head_count // seq_count
    head_start = seq_index * local_heads
    dt_local = lax.dynamic_slice_in_dim(dt_full, head_start, local_heads).astype(jnp.float32)
    alog_local = lax.dynamic_slice_in_dim(alog_full, head_start, local_heads).astype(jnp.float32)
    skip_local = lax.dynamic_slice_in_dim(skip_full, head_start, local_heads).astype(jnp.float32)

    def scan_local(x_vals, dt_vals, b_vals, c_vals, bias_vals, decay_vals, skip_vals):
        return scan_heads(
            x_vals, dt_vals, b_vals, c_vals, ids_full, bias_vals, decay_vals, skip_vals, BLOCK
        )

    scanned, scan_pull = jax.vjp(
        scan_local,
        head_x.astype(jnp.float32),
        head_dt.astype(jnp.float32),
        bc_full[:, :state_dim].astype(jnp.float32),
        bc_full[:, state_dim:].astype(jnp.float32),
        dt_local,
        alog_local,
        skip_local,
    )
    y_rows = lax.all_to_all(
        scanned.astype(jnp.bfloat16), "seq", split_axis=0, concat_axis=1, tiled=True
    )
    gated_f, gated_pull = jax.vjp(
        gated_norm,
        y_rows.astype(jnp.float32),
        gate_part.astype(jnp.float32),
        gate_full.astype(jnp.float32),
    )
    gated = gated_f.astype(jnp.bfloat16)
    output = (residual_in + jnp.dot(gated, w_out, preferred_element_type=jnp.float32)).astype(
        jnp.bfloat16
    )
    grad_out = cotangent[0]
    grad_wout = lax.dot_general(
        gated, grad_out, (((0,), (0,)), ((), ())), preferred_element_type=jnp.float32
    )
    grad_gated = lax.dot_general(
        grad_out, w_out, (((1,), (1,)), ((), ())), preferred_element_type=jnp.float32
    )
    grad_y, grad_gate_part, grad_gate_gain = gated_pull(grad_gated)
    head_grad = lax.all_to_all(
        grad_y.astype(jnp.bfloat16), "seq", split_axis=1, concat_axis=0, tiled=True
    )
    grad_hx, grad_hdt, grad_b, grad_c, grad_bias, grad_decay, grad_skipped = scan_pull(
        head_grad.astype(jnp.float32)
    )
    back_x, back_dt = (
        lax.all_to_all(
            grad_hx.astype(jnp.bfloat16), "seq", split_axis=0, concat_axis=1, tiled=True
        ),
        lax.all_to_all(
            grad_hdt.astype(jnp.bfloat16), "seq", split_axis=0, concat_axis=1, tiled=True
        ),
    )
    grad_bc = lax.psum_scatter(
        jnp.concatenate([grad_b, grad_c], axis=1).astype(jnp.bfloat16),
        "seq",
        scatter_dimension=0,
        tiled=True,
    ).astype(jnp.float32)
    grad_act = jnp.concatenate([back_x.astype(jnp.float32), grad_bc], axis=1)
    grad_ext, grad_convw, grad_convb = conv_pull(grad_act)
    rim_back = shifted(grad_ext[: tap_count - 1], "seq", -1)
    grad_conv_in = jnp.concatenate(
        [grad_ext[tap_count - 1 : tok_rows], grad_ext[tok_rows:] + rim_back]
    )
    grad_proj = jnp.concatenate(
        [grad_gate_part, grad_conv_in, back_dt.astype(jnp.float32)], axis=1
    ).astype(jnp.bfloat16)
    grad_win = lax.dot_general(
        normed, grad_proj, (((0,), (0,)), ((), ())), preferred_element_type=jnp.float32
    )
    grad_normed = lax.dot_general(
        grad_proj, w_in, (((1,), (1,)), ((), ())), preferred_element_type=jnp.float32
    )
    grad_resid, grad_norm = norm_pull(grad_normed)
    grad_input = grad_resid + grad_out.astype(jnp.float32)

    def place_heads(values):
        return lax.dynamic_update_slice_in_dim(
            jnp.zeros((head_count,), jnp.float32), values, head_start, 0
        )

    grad_dtb = place_heads(grad_bias)
    grad_alog = place_heads(grad_decay)
    grad_skip = place_heads(grad_skipped)
    summed = lax.psum(
        (
            grad_win,
            grad_wout,
            grad_convw,
            grad_convb,
            grad_dtb,
            grad_alog,
            grad_skip,
            grad_norm,
            grad_gate_gain,
        ),
        "seq",
    )
    shards = (
        lax.psum_scatter(summed[0], "wsh", scatter_dimension=0, tiled=True),
        lax.psum_scatter(summed[1], "wsh", scatter_dimension=0, tiled=True),
        lax.psum_scatter(summed[2], "wsh", scatter_dimension=1, tiled=True),
        lax.psum_scatter(summed[3], "wsh", scatter_dimension=0, tiled=True),
        lax.psum_scatter(summed[4], "wsh", scatter_dimension=0, tiled=True),
        lax.psum_scatter(summed[5], "wsh", scatter_dimension=0, tiled=True),
        lax.psum_scatter(summed[6], "wsh", scatter_dimension=0, tiled=True),
        lax.psum_scatter(summed[7], "wsh", scatter_dimension=0, tiled=True),
        lax.psum_scatter(summed[8], "wsh", scatter_dimension=0, tiled=True),
    )
    return (
        output[None],
        grad_input[None],
        shards[0],
        shards[1],
        shards[2],
        shards[3],
        shards[4],
        shards[5],
        shards[6],
        shards[7],
        shards[8],
    )


def solution(mesh):
    in_specs = (
        P("wsh", "seq", None),
        P("wsh", "seq"),
        P("wsh", None),
        P("wsh", None),
        P(None, "wsh"),
        P("wsh"),
        P("wsh"),
        P("wsh"),
        P("wsh"),
        P("wsh"),
        P("wsh"),
        P("wsh", "seq", None),
    )
    out_specs = (
        P("wsh", "seq", None),
        P("wsh", "seq", None),
        P("wsh", None),
        P("wsh", None),
        P(None, "wsh"),
        P("wsh"),
        P("wsh"),
        P("wsh"),
        P("wsh"),
        P("wsh"),
        P("wsh"),
    )
    return jax.shard_map(local, mesh=mesh, in_specs=in_specs, out_specs=out_specs, check_vma=False)
```

profile of v0, /device:TPU:0, one launch (start us, length us, event | category | flops | bytes accessed | tf_op | source)
XLA Modules:
  0.0 1654.8 jit_solution(10845675449132418567)
XLA Ops:
  8.6 12.6 all-gather
  21.3 31.8 %all-gather.1 = bf16[4,576,4]{1,2,0:T(4,128)(2,1)S(1)} all-gather(bf16[1,576,4]{1,2,0:T(4,128)(2,1)} %bitcast.442), channel_id=1, replica_groups=mesh['seq'=8,'wsh'=4] {'wsh'}, dimensions={0}, use_global_device_ids=true | all-gather | bytes 23040 | tf_op jit(solution)/shard_map/all_gather | solution.py:110
  53.2 9.0 all_gather.37
  63.9 107.3 %all-gather.7.cloned.1.call-done = bf16[1024,4384]{0,1:T(8,128)(2,1)} async-done(((bf16[256,4384]{0,1:T(8,128)(2,1)}), bf16[1024,4384]{0,1:T(8,128)(2,1)}) %all-gather.7.cloned.1.call-update) | async-done | bytes 8978448 | tf_op jit(solution)/shard_map/all_gather | solution.py:108
  171.3 9.2 convolution_convert_fusion
  187.3 9.5 all-reduce.24
  222.2 27.8 %all-to-all-done.1 = bf16[512,8,256]{0,2,1:T(8,128)(2,1)S(1)} async-done(((bf16[512,8,256]{0,2,1:T(8,128)(2,1)}), bf16[512,8,256]{0,2,1:T(8,128)(2,1)S(1)}, u32[]{:S(2)}, u32[]{:S(2)}) %all-to-all-start.1) | async-done | bytes 2097184 | tf_op jit(solution)/shard_map/all_to_all | solution.py:149
  262.3 271.7 %while.40 = (s32[]{:T(128)}, f32[4,64,128]{2,1,0:T(8,128)S(1)}, f32[8,512,4,64]{1,0,3,2:T(8,128)}, f32[8,4,64,128]{3,2,1,0:T(8,128)}, f32[8,512,4]{1,2,0:T(4,128...) while((s32[]{:T(128)}, f32[4,64,128]{2,1,0:T(8,128)S(1)}, ...), condition=%wide.region_4.5_spmd.clone, body=%wide.region_1.4_spmd.clone.sunk | while | flops 1616420864 | bytes 9202848 | solution.py:88
  269.3 6.4 fusion.210
  284.8 11.5 dynamic_update_slice.83
  303.3 6.3 fusion.210
  318.8 11.5 dynamic_update_slice.83
  337.2 6.3 fusion.210
  352.7 11.5 dynamic_update_slice.83
  371.2 6.3 fusion.210
  386.7 11.5 dynamic_update_slice.83
  405.1 6.3 fusion.210
  420.6 11.5 dynamic_update_slice.83
  439.1 6.3 fusion.210
  454.6 11.5 dynamic_update_slice.83
  473.0 6.3 fusion.210
  488.5 11.5 dynamic_update_slice.83
  507.0 6.3 fusion.210
  522.5 11.5 dynamic_update_slice.83
  543.2 11.9 all-gather.2
  555.1 14.6 all-to-all-done.2
  578.1 6.2 multiply_reduce_fusion.11
  584.4 7.0 multiply_reduce_fusion.7
  603.2 26.5 %all-to-all-done.3 = bf16[512,8,256]{0,2,1:T(8,128)(2,1)S(1)} async-done(((bf16[512,8,256]{0,2,1:T(8,128)(2,1)}), bf16[512,8,256]{0,2,1:T(8,128)(2,1)S(1)}, u32[]{:S(2)}, u32[]{:S(2)}) %all-to-all-start.3) | async-done | bytes 2097184 | tf_op jit(solution)/shard_map/all_to_all | solution.py:195
  638.3 369.4 %while.41 = (s32[]{:T(128)}, f32[4,64,128]{2,1,0:T(8,128)S(1)}, f32[8,512,4]{1,2,0:T(4,128)}, f32[8,512,4,64]{1,3,2,0:T(8,128)}, bf16[8,512,128]{2,1,0:T(8,128)(...) while((s32[]{:T(128)}, f32[4,64,128]{2,1,0:T(8,128)S(1)}, ...), condition=%wide.region_19.20_spmd.clone, body=%wide.region_7.19_spmd.clone.sunk | while | flops 3843487744 | bytes 28192232 | solution.py:88
  672.5 6.0 fusion.236
  718.7 6.0 fusion.236
  764.8 5.9 fusion.236
  810.9 5.9 fusion.236
  857.0 6.0 fusion.236
  903.1 6.0 fusion.236
  995.3 5.9 fusion.236
  1011.0 7.9 fusion.115
  1050.1 26.4 %all-to-all-done.4 = bf16[8,512,256]{1,2,0:T(8,128)(2,1)} async-done(((bf16[8,512,256]{1,2,0:T(8,128)(2,1)}), bf16[8,512,256]{1,2,0:T(8,128)(2,1)}, u32[]{:S(2)}, u32[]{:S(2)}) %all-to-all-start.4) | async-done | bytes 2097184 | tf_op jit(solution)/shard_map/all_to_all | solution.py:202
  1080.5 12.2 multiply_reduce_fusion.6
  1101.4 10.3 fusion.119
  1115.9 80.4 %reduce-scatter.11.cloned.1.call-done = f32[512,1024]{1,0:T(8,128)} async-done(((f32[2048,1024]{1,0:T(8,128)}), f32[512,1024]{1,0:T(8,128)}) %reduce-scatter.11.cloned.1.call-update) | async-done | bytes 2097168 | tf_op jit(solution)/shard_map/reduce_scatter | solution.py:257
  1196.3 302.1 %reduce-scatter.9.cloned.1.call-done = f32[256,4384]{0,1:T(8,128)} async-done(((f32[1024,4384]{0,1:T(8,128)}), f32[256,4384]{0,1:T(8,128)}) %reduce-scatter.9.cloned.1.call-update) | async-done | bytes 4489232 | tf_op jit(solution)/shard_map/reduce_scatter | solution.py:256
  1498.4 7.2 fusion.114
  1510.0 11.8 fusion.107
  1521.8 18.7 %all-reduce.23 = (f32[2304]{0:T(1024)S(1)}, f32[32]{0:T(128)S(1)}, f32[32]{0:T(128)S(1)}, f32[32]{0:T(128)S(1)}, f32[1024]{0:T(1024)S(1)}, /*index=5*/f32[2048]{0:T(1024)S(1)}) all-reduce(f32[2304]{0:T(1024)S(1)} %get-tuple-element.698, f32[32]{0:T(128)S(1)} %dynamic_update_slice.61, ...), channel_id=6, replica_groups=mesh['seq'=8,'wsh'=4] {'wsh'}, use_global_device_ids=true, to_apply=%region_35.36.clone | all-reduce | flops 5472 | bytes 43776
  1545.6 24.4 %all-reduce.21 = (f32[4,576]{1,0:T(4,128)}, f32[576]{0:T(1024)}, f32[8]{0:T(128)}, f32[8]{0:T(128)}, f32[8]{0:T(128)}, /*index=5*/f32[256]{0:T(256)}, f32[512]{0:T(512)}) all-reduce(f32[4,576]{1,0:T(4,128)S(1)} %copy.188, f32[576]{0:T(1024)S(1)} %dynamic-slice.5, f32[8]{0:T(128)S(1)} %dynamic-slice.7, ...), channel_id=1, replica_groups=mesh['seq'=8,'wsh'=4] {'seq'}, use_global_device_ids=true, to_apply=%region_31.32 | all-reduce | flops 3672 | bytes 29376 | tf_op jit(solution)/shard_map/psum | solution.py:241
  1570.0 71.6 %all-reduce.27.cloned.1.call-done = (f32[256,4384]{0,1:T(8,128)}, f32[512,1024]{1,0:T(8,128)}) async-done(((f32[256,4384]{0,1:T(8,128)}, f32[512,1024]{1,0:T(8,128)}), (f32[256,4384]{0,1:T(8,128)}, f32[512,1024]{1,0:T(8,128)})) %all-reduce.27.cloned.1.call-update) | async-done | bytes 6586384 | tf_op jit(solution)/shard_map/psum | solution.py:241
  (843 shorter events, 602.4 us)
Async XLA Ops:
  7.2 164.1 %all-gather.7.cloned.1.call-start = ((), (), s32[]{:S(2)}) async-start(), calls=%async_computation.10 | async-start | bytes 11223040 | tf_op jit(solution)/shard_map/all_gather | solution.py:108
  7.9 249.8 %all-gather.9.cloned.1.call-start = ((), (), s32[]{:S(2)}) async-start(), calls=%async_computation.11 | async-start | bytes 2359296 | tf_op jit(solution)/shard_map/all_gather | solution.py:152
  21.3 159.2 %copy-start.47 = (f32[4,1,256]{2,1,0:T(1,128)}, f32[4,1,256]{2,1,0:T(1,128)S(1)}, u32[]{:S(2)}) copy-start(f32[4,1,256]{2,1,0:T(1,128)S(1)} %convert_element_type.252) | copy-start | bytes 12292
  63.8 116.7 %copy-start.45 = (f32[512]{0:T(512)}, f32[512]{0:T(512)S(1)}, u32[]{:S(2)}) copy-start(f32[512]{0:T(512)S(1)} %fusion.110) | copy-start | bytes 6148
  63.8 116.7 %copy-start.51 = (f32[512]{0:T(512)}, f32[512]{0:T(512)S(1)}, u32[]{:S(2)}) copy-start(f32[512]{0:T(512)S(1)} %fusion.134) | copy-start | bytes 6148
  63.9 133.4 %copy-start.37 = (f32[512]{0:T(512)}, f32[512]{0:T(512)S(1)}, u32[]{:S(2)}) copy-start(f32[512]{0:T(512)S(1)} %get-tuple-element.812) | copy-start | bytes 6148
  63.9 133.5 %copy-start.39 = (f32[512]{0:T(512)}, f32[512]{0:T(512)S(1)}, u32[]{:S(2)}) copy-start(f32[512]{0:T(512)S(1)} %get-tuple-element.813) | copy-start | bytes 6148
  63.9 133.5 %copy-start.41 = (f32[512]{0:T(512)}, f32[512]{0:T(512)S(1)}, u32[]{:S(2)}) copy-start(f32[512]{0:T(512)S(1)} %get-tuple-element.814) | copy-start | bytes 6148
  171.3 13.1 copy-start.58
  171.3 15.0 copy-start.63
  171.3 15.3 copy-start.64
  171.3 15.5 copy-start.65
  171.3 15.8 copy-start.59
  182.8 14.1 slice-start
  182.8 14.0 collective-permute-start
  184.3 13.0 copy-start.29
  184.3 13.0 copy-start.31
  184.3 13.0 copy-start.33
  184.4 13.0 copy-start.35
  196.8 23.9 %copy-start.61 = (bf16[32]{0:T(256)(128)(2,1)}, bf16[32]{0:T(256)(128)(2,1)S(1)}, u32[]{:S(2)}) copy-start(bf16[32]{0:T(256)(128)(2,1)S(1)} %get-tuple-element.769) | copy-start | bytes 196
  204.3 9.4 all-to-all-start
  213.6 37.6 %copy-start.23 = (bf16[512,8,4]{0,2,1:T(4,128)(2,1)}, bf16[512,8,4]{0,2,1:T(4,128)(2,1)S(1)}, u32[]{:S(2)}) copy-start(bf16[512,8,4]{0,2,1:T(4,128)(2,1)S(1)} %all-to-all-done) | copy-start | bytes 98308
  213.6 36.4 %all-to-all-start.1 = ((bf16[512,8,256]{0,2,1:T(8,128)(2,1)}), bf16[512,8,256]{0,2,1:T(8,128)(2,1)S(1)}, u32[]{:S(2)}, u32[]{:S(2)}) async-start(bf16[512,8,256]{0,2,1:T(8,128)(2,1)} %bitcast.407), calls=%async_computation.1 | async-start | bytes 4194304 | tf_op jit(solution)/shard_map/all_to_all | solution.py:149
  217.8 366.5 %all-gather.11.cloned.1.call-start = ((), (), s32[]{:S(2)}) async-start(), calls=%async_computation.12 | async-start | bytes 5242880 | tf_op jit(solution)/shard_map/all_gather | solution.py:109
  220.7 313.3 %copy-start.49 = (f32[256]{0:T(256)}, f32[256]{0:T(256)S(1)}, u32[]{:S(2)}) copy-start(f32[256]{0:T(256)S(1)} %mul.804) | copy-start | bytes 3076
  220.8 36.9 %copy-start.56 = (f32[4]{0:T(128)}, f32[4]{0:T(128)S(1)}, u32[]{:S(2)}) copy-start(f32[4]{0:T(128)S(1)} %fusion.136) | copy-start | bytes 52
  220.9 36.8 %copy-start.54 = (f32[4]{0:T(128)}, f32[4]{0:T(128)S(1)}, u32[]{:S(2)}) copy-start(f32[4]{0:T(128)S(1)} %dynamic-slice_convert_fusion.1) | copy-start | bytes 52
  222.2 35.4 %copy-start.21 = (f32[8,512,4]{1,2,0:T(4,128)}, f32[8,512,4]{1,2,0:T(4,128)S(1)}, u32[]{:S(2)}) copy-start(f32[8,512,4]{1,2,0:T(4,128)S(1)} %get-tuple-element.780) | copy-start | bytes 196612
  250.0 284.0 %copy-start.6 = (bf16[512,8,256]{0,2,1:T(8,128)(2,1)}, bf16[512,8,256]{0,2,1:T(8,128)(2,1)S(1)}, u32[]{:S(2)}) copy-start(bf16[512,8,256]{0,2,1:T(8,128)(2,1)S(1)} %all-to-all-done.1) | copy-start | bytes 6291460
  539.5 30.2 %all-to-all-start.2 = ((bf16[8,512,256]{1,2,0:T(8,128)(2,1)}), bf16[8,512,256]{1,2,0:T(8,128)(2,1)S(1)}, u32[]{:S(2)}, u32[]{:S(2)}) async-start(bf16[8,512,256]{1,2,0:T(8,128)(2,1)} %copy.172), calls=%async_computation.2 | async-start | bytes 4194304 | tf_op jit(solution)/shard_map/all_to_all | solution.py:174
  555.1 36.3 %copy-start.27 = (f32[4,1,512]{2,1,0:T(1,128)}, f32[4,1,512]{2,1,0:T(1,128)S(1)}, u32[]{:S(2)}) copy-start(f32[4,1,512]{2,1,0:T(1,128)S(1)} %convert_element_type.254) | copy-start | bytes 24580
  599.5 30.2 %all-to-all-start.3 = ((bf16[512,8,256]{0,2,1:T(8,128)(2,1)}), bf16[512,8,256]{0,2,1:T(8,128)(2,1)S(1)}, u32[]{:S(2)}, u32[]{:S(2)}) async-start(bf16[512,8,256]{0,2,1:T(8,128)(2,1)} %bitcast.408), calls=%async_computation.3 | async-start | bytes 4194304 | tf_op jit(solution)/shard_map/all_to_all | solution.py:195
  603.1 477.3 %reduce-scatter.7.cloned.1.call-start = ((), (), s32[]{:S(2)}) async-start(), calls=%async_computation.13 | async-start | bytes 2359296 | tf_op jit(solution)/shard_map/reduce_scatter | solution.py:209
  1011.0 185.3 %reduce-scatter.11.cloned.1.call-start = ((), (), s32[]{:S(2)}) async-start(), calls=%async_computation.15 | async-start | bytes 10485760 | tf_op jit(solution)/shard_map/reduce_scatter | solution.py:257
  1034.6 10.9 all-to-all-start.5
  1045.5 34.9 %copy-start.38 = (f32[512]{0:T(512)S(1)}, f32[512]{0:T(512)}, u32[]{:S(2)}) copy-start(f32[512]{0:T(512)} %copy-done.37) | copy-start | bytes 6148
  1045.5 34.9 %copy-start.40 = (f32[512]{0:T(512)S(1)}, f32[512]{0:T(512)}, u32[]{:S(2)}) copy-start(f32[512]{0:T(512)} %copy-done.39) | copy-start | bytes 6148
  1045.5 34.9 %copy-start.42 = (f32[512]{0:T(512)S(1)}, f32[512]{0:T(512)}, u32[]{:S(2)}) copy-start(f32[512]{0:T(512)} %copy-done.41) | copy-start | bytes 6148
  1045.5 31.0 %all-to-all-start.4 = ((bf16[8,512,256]{1,2,0:T(8,128)(2,1)}), bf16[8,512,256]{1,2,0:T(8,128)(2,1)}, u32[]{:S(2)}, u32[]{:S(2)}) async-start(bf16[8,512,256]{1,2,0:T(8,128)(2,1)} %copy.178), calls=%async_computation.4 | async-start | bytes 4194304 | tf_op jit(solution)/shard_map/all_to_all | solution.py:202
  1049.9 448.5 %reduce-scatter.9.cloned.1.call-start = ((), (), s32[]{:S(2)}) async-start(), calls=%async_computation.14 | async-start | bytes 22446080 | tf_op jit(solution)/shard_map/reduce_scatter | solution.py:256
  1080.4 12.2 copy-start.30
  1080.4 12.2 copy-start.32
  1080.5 12.2 copy-start.34
  1094.6 4.0 collective-permute-start.1
  1111.7 432.8 %reduce-scatter.13.cloned.1.call-start = ((), (), s32[]{:S(2)}) async-start(), calls=%async_computation.16 | async-start | bytes 1474560
  1113.3 528.3 %all-reduce.27.cloned.1.call-start = ((), (), s32[]{:S(2)}) async-start(), calls=%async_computation.17 | async-start | bytes 13172736 | tf_op jit(solution)/shard_map/psum | solution.py:241
  1510.0 31.0 %copy-start.46 = (f32[512]{0:T(512)S(1)}, f32[512]{0:T(512)}, u32[]{:S(2)}) copy-start(f32[512]{0:T(512)} %copy-done.45) | copy-start | bytes 6148
  1510.0 31.0 %copy-start.16 = (bf16[1,512,1024]{2,1,0:T(8,128)(2,1)S(1)}, bf16[1,512,1024]{2,1,0:T(8,128)(2,1)}, u32[]{:S(2)}) copy-start(bf16[1,512,1024]{2,1,0:T(8,128)(2,1)} %param.16) | copy-start | bytes 3145732
  (64 other events, 390.2 us)
Sparse Core Ops, SparseCore 0:
  9.5 161.6 all-gather.6
  203.7 38.2 all-gather.8
  243.6 79.8 all-gather.10
  1011.1 38.2 reduce-scatter.6
  1051.6 144.6 reduce-scatter.10
  1198.5 299.8 reduce-scatter.8
  1500.7 30.4 reduce-scatter.12
  1534.7 106.8 all-reduce.26
where the time goes:
time: 1670 us; the launch traced here: 1650 us
  waiting for transfers between devices  658 us (39%)
  matrix products  320 us (19%)
  local copies, waits for them, and re-layouts  300 us (18%)
  other arithmetic  211 us (13%)
  blocking collectives  118 us (7%)
  starting transfers between devices  26.4 us (2%)
  between operations  19.3 us (1%)
    reduce_scatter x1, waiting for transfers between devices, local(): lax.psum_scatter(summed[0], 'wsh', scatter_dimension=0, tiled=True)  302 us
    dot_general x24, matrix products, one_block(): jnp.einsum('hts,shp->thp', mixed_kernel, scaled_part, precision=highest)  145 us
    all_gather x1, waiting for transfers between devices, local(): lax.all_gather(in_weight, 'wsh', axis=0, tiled=True)  107 us
    dynamic_update_slice x24, local copies, waits for them, and re-layouts, scan_heads(): ignored, outputs = lax.scan(jax.checkpoint(one_block), initial, pieces)  101 us
    another operation x60, other arithmetic  90.8 us
    reduce_scatter x1, waiting for transfers between devices, local(): lax.psum_scatter(summed[1], 'wsh', scatter_dimension=0, tiled=True)  80.4 us
    psum x1, waiting for transfers between devices, local(): lax.psum((grad_win, grad_wout, grad_convw, grad_convb, grad_dtb, grad_alo...  71.6 us
    dot_general x32, matrix products, one_block(): scores = jnp.dot(c_part, b_part.T, precision=highest)  64.9 us
  transfers between devices with their start and end apart: 16, of which 8 were waited for; matrix products, arithmetic and copies ran while one was open for 25% of the time, Pallas kernels for 0%

commit v1 on v0

v1 whole, which is shorter than its diff:
```python
import functools

import jax
import jax.numpy as jnp
from jax import lax
from jax.experimental import pallas as pl
from jax.experimental.pallas import tpu as pltpu
from jax.sharding import PartitionSpec as P

epsilon = 1e-05
bf16, f32 = jnp.bfloat16, jnp.float32
LB = 128
GW = 256
HALO = 16
TAPS = 4
NEG = -1e30


def mm(a, b):
    return jnp.dot(a, b, preferred_element_type=f32)


def mm_nt(a, b):
    return lax.dot_general(a, b, (((1,), (1,)), ((), ())), preferred_element_type=f32)


def mm_tn(a, b):
    return lax.dot_general(a, b, (((0,), (0,)), ((), ())), preferred_element_type=f32)


def split2(v):
    hi = v.astype(bf16)
    return hi, (v - hi.astype(f32)).astype(bf16)


def split3(v):
    hi = v.astype(bf16)
    rest = v - hi.astype(f32)
    mid = rest.astype(bf16)
    return hi, mid, (rest - mid.astype(f32)).astype(bf16)


def pick(base, width, each):
    row = lax.broadcasted_iota(jnp.int32, (128, width), 0)
    col = lax.broadcasted_iota(jnp.int32, (128, width), 1) // each
    return jnp.where(row == base + col, 1.0, 0.0).astype(bf16)


def lane_sums(sel, v):
    hi, lo = split2(v)
    return mm_nt(sel, hi) + mm_nt(sel, lo)


def head_rows(hd):
    row = lax.broadcasted_iota(jnp.int32, (8, GW), 0)
    col = lax.broadcasted_iota(jnp.int32, (8, GW), 1) // hd
    return jnp.where(row == col, 1.0, 0.0).astype(bf16)


def scan_lanes(v, reverse):
    width = v.shape[1]
    lane = lax.broadcasted_iota(jnp.int32, v.shape, 1)
    s = 1
    while s < width:
        if reverse:
            v = v + jnp.where(lane < width - s, pltpu.roll(v, width - s, 1), 0.0)
        else:
            v = v + jnp.where(lane >= s, pltpu.roll(v, s, 1), 0.0)
        s *= 2
    return v


def sigmoid(v):
    return 1.0 / (1.0 + jnp.exp(-v))


def softplus(v):
    return jnp.maximum(v, 0.0) + jnp.log1p(jnp.exp(-jnp.abs(v)))


RC = 32


def fill_extended(ext, cin, rows):
    ext[0:8] = cin[rows + HALO - 8 : rows + HALO].astype(f32)
    ext[8 : 8 + rows] = cin[0:rows].astype(f32)


def conv_pre(ext, cw, masks, r):
    pre = cw[TAPS : TAPS + 1] + ext[8 + r : 8 + r + RC] * cw[TAPS - 1 : TAPS]
    for k in range(TAPS - 1):
        off = 8 - (TAPS - 1) + k + r
        pre = pre + ext[off : off + RC] * cw[k : k + 1] * masks[r : r + RC, k : k + 1]
    return pre


def kernel_a(rows, hd, cin, cw, masks, mrow, dtt, hp, xo, bco, so, cumo, stepo, colo, ext, cols, act):
    i = pl.program_id(0)
    fill_extended(ext, cin, rows)
    for r in range(0, rows, RC):
        pre = conv_pre(ext, cw, masks, r)
        act[r : r + RC] = (pre * sigmoid(pre)).astype(bf16)

    @pl.when(i == 0)
    def _():
        bco[...] = act[...]
        step = softplus(dtt[...] + hp[:, 0:1])
        cum = scan_lanes(-jnp.exp(hp[:, 1:2]) * step, False)
        stepo[...] = step
        cumo[...] = cum
        n = rows // LB
        w_in, w_end = [], []
        for c in range(n):
            own = cum[:, c * LB : (c + 1) * LB]
            if c == 0:
                w_in.append(jnp.exp(own))
            else:
                w_in.append(jnp.exp(own - cum[:, c * LB - 1 : c * LB]))
            w_end.append(jnp.exp(own[:, LB - 1 : LB] - own))
        w_in = jnp.concatenate(w_in, 1) * mrow[0:1]
        w_end = jnp.concatenate(w_end, 1) * mrow[1:2]
        w_dev = jnp.exp(cum) * mrow[2:3]
        w_all = jnp.exp(cum[:, rows - 1 : rows] - cum) * mrow[3:4] * step
        first = jnp.concatenate([cum, step], 0).T
        for q, part in enumerate(split3(first)):
            colo[q] = part
        pairs = ((w_in, w_end), (w_end * step, w_all), (w_dev, jnp.zeros_like(w_dev)))
        for q, (one, two) in enumerate(pairs):
            hi, lo = split2(jnp.concatenate([one, two], 0).T)
            colo[3 + 2 * q] = hi
            colo[4 + 2 * q] = lo
        cols[0] = colo[5]
        cols[1] = colo[6]
        cols[2] = colo[7]
        cols[3] = colo[8]
        so[...] = jnp.zeros_like(so)

    @pl.when(i > 0)
    def _():
        g = i - 1
        x = act[...]
        xo[...] = x
        sel = pick(64 + 8 * g, GW, hd)
        wexp = mm(cols[0], sel) + mm(cols[1], sel)
        xw = (x.astype(f32) * wexp).astype(bf16)
        so[0, 0:128] = mm_tn(bco[:, 0:128], xw).astype(bf16)
        sel = pick(8 * g, GW, hd)
        dev = mm(cols[2, rows - 16 : rows], sel) + mm(cols[3, rows - 16 : rows], sel)
        hi, lo = split2(dev[15:16])
        so[0, 128:144] = jnp.concatenate([hi, lo, jnp.zeros((14, GW), bf16)], 0)


def call_a(pc, cw, masks, mrow, dtt, hp, rows, di, hd):
    ng = di // GW
    nb = ng + 1
    col = lambda i: (0, (i + ng) % nb)
    grp = lambda i: (0, jnp.maximum(i - 1, 0))
    full = lambda i: (0, 0)
    return pl.pallas_call(
        functools.partial(kernel_a, rows, hd),
        grid=(nb,),
        in_specs=[
            pl.BlockSpec((rows + HALO, GW), col),
            pl.BlockSpec((8, GW), col),
            pl.BlockSpec((rows, 8), full),
            pl.BlockSpec((8, rows), full),
            pl.BlockSpec((64, rows), full),
            pl.BlockSpec((64, 8), full),
        ],
        out_specs=[
            pl.BlockSpec((rows, GW), grp),
            pl.BlockSpec((rows, GW), full),
            pl.BlockSpec((1, 144, GW), lambda i: (jnp.maximum(i - 1, 0), 0, 0)),
            pl.BlockSpec((64, rows), full),
            pl.BlockSpec((64, rows), full),
            pl.BlockSpec((9, rows, 128), lambda i: (0, 0, 0)),
        ],
        out_shape=[
            jax.ShapeDtypeStruct((rows, di), bf16),
            jax.ShapeDtypeStruct((rows, GW), bf16),
            jax.ShapeDtypeStruct((ng, 144, GW), bf16),
            jax.ShapeDtypeStruct((64, rows), f32),
            jax.ShapeDtypeStruct((64, rows), f32),
            jax.ShapeDtypeStruct((9, rows, 128), bf16),
        ],
        scratch_shapes=[
            pltpu.VMEM((rows + 8, GW), f32),
            pltpu.VMEM((4, rows, 128), bf16),
            pltpu.VMEM((rows, GW), bf16),
        ],
        compiler_params=pltpu.CompilerParams(dimension_semantics=("arbitrary",)),
        cost_estimate=pl.CostEstimate(flops=400000000, bytes_accessed=6000000, transcendentals=2400000),
        name="conv_state",
    )(pc, cw, masks, mrow, dtt, hp)


def kernel_f(n, recv, sin, dec):
    state = jnp.zeros((128, GW), f32)
    for i in range(n):
        sin[i] = state.astype(bf16)
        d = recv[i, 128:129].astype(f32) + recv[i, 129:130].astype(f32)
        dec[i] = jnp.broadcast_to(d, (8, GW))
        state = state * d + recv[i, 0:128].astype(f32)


def call_f(recv):
    n = recv.shape[0]
    return pl.pallas_call(
        functools.partial(kernel_f, n),
        out_shape=[
            jax.ShapeDtypeStruct((n, 128, GW), bf16),
            jax.ShapeDtypeStruct((n, 8, GW), f32),
        ],
        name="join_forward",
    )(recv)


def kernel_g(n, recv, dec, gin):
    adj = jnp.zeros((128, GW), f32)
    for i in reversed(range(n)):
        gin[i] = adj.astype(bf16)
        adj = adj * dec[i, 0:1] + recv[i].astype(f32)


def call_g(recv, dec):
    n = recv.shape[0]
    return pl.pallas_call(
        functools.partial(kernel_g, n),
        out_shape=jax.ShapeDtypeStruct((n, 128, GW), bf16),
        name="join_backward",
    )(recv, dec)


def negmask(masks, mrow, c, flip):
    rows = slice(c * LB, (c + 1) * LB)
    same = masks[rows, 3:4] == mrow[4:5, rows]
    a = lax.broadcasted_iota(jnp.int32, (LB, LB), 0)
    b = lax.broadcasted_iota(jnp.int32, (LB, LB), 1)
    order = (a <= b) if flip else (b <= a)
    return jnp.where(same & order, 0.0, NEG)


def half_masks(hd):
    lane = lax.broadcasted_iota(jnp.int32, (LB, 128), 1)
    low = jnp.where(lane < hd, 1.0, 0.0).astype(bf16)
    high = jnp.where(lane < hd, 0.0, 1.0).astype(bf16)
    return low, high


def kernel_b(rows, hd, g0, x, bc, cols, cumt, stept, masks, mrow, yo, score, neg, cumb, st):
    i = pl.program_id(0)
    g = g0 + i
    n = rows // LB

    @pl.when(i == 0)
    def _():
        for c in range(n):
            r = slice(c * LB, (c + 1) * LB)
            score[c] = mm_nt(bc[r, 128:256], bc[r, 0:128])
            neg[c] = negmask(masks, mrow, c, False)

    sel = pick(8 * g, 4 * LB, LB)
    cumb[...] = mm(cols[0], sel) + mm(cols[1], sel) + mm(cols[2], sel)
    sel = pick(8 * g, GW, hd)
    low, high = half_masks(hd)
    for c in range(n):
        r = slice(c * LB, (c + 1) * LB)
        outs = []
        for p in range(2):
            mats = []
            for j in range(2):
                h = 2 * p + j
                diff = cumb[r, h * LB : (h + 1) * LB] - cumt[h : h + 1, r]
                m = jnp.exp(diff + neg[c]) * score[c] * stept[h : h + 1, r]
                mats.append(m.astype(bf16))
            xp = x[r, 128 * p : 128 * (p + 1)]
            outs.append(mm(jnp.concatenate(mats, 1), jnp.concatenate([xp * low, xp * high], 0)))
        y = jnp.concatenate(outs, 1)
        if c > 0:
            w_in = mm(cols[3, r], sel) + mm(cols[4, r], sel)
            y = y + mm(bc[r, 128:256], st[...].astype(bf16)) * w_in
        yo[r] = y
        if c < n - 1:
            w_end = mm(cols[5, r], sel) + mm(cols[6, r], sel)
            fresh = mm_tn(bc[r, 0:128], (x[r].astype(f32) * w_end).astype(bf16))
            if c > 0:
                fresh = fresh + st[...] * w_in[LB - 1 : LB]
            st[...] = fresh


def call_b(x, bc, cols, cumt, stept, masks, mrow, rows, hd, g0, count):
    n = rows // LB
    grp = lambda i: (0, g0 + i)
    row = lambda i: (g0 + i, 0)
    full = lambda i: (0, 0)
    return pl.pallas_call(
        functools.partial(kernel_b, rows, hd, g0),
        grid=(count,),
        in_specs=[
            pl.BlockSpec((rows, GW), grp),
            pl.BlockSpec((rows, GW), full),
            pl.BlockSpec((9, rows, 128), lambda i: (0, 0, 0)),
            pl.BlockSpec((8, rows), row),
            pl.BlockSpec((8, rows), row),
            pl.BlockSpec((rows, 8), full),
            pl.BlockSpec((8, rows), full),
        ],
        out_specs=pl.BlockSpec((rows, GW), lambda i: (0, i)),
        out_shape=jax.ShapeDtypeStruct((rows, count * GW), f32),
        scratch_shapes=[
            pltpu.VMEM((n, LB, LB), f32),
            pltpu.VMEM((n, LB, LB), f32),
            pltpu.VMEM((rows, 4 * LB), f32),
            pltpu.VMEM((128, GW), f32),
        ],
        compiler_params=pltpu.CompilerParams(dimension_semantics=("arbitrary",)),
        cost_estimate=pl.CostEstimate(flops=800000000, bytes_accessed=4000000, transcendentals=1000000),
        name="scan_forward",
    )(x, bc, cols, cumt, stept, masks, mrow)


SR = 16


def kernel_c(ng, hd, ya, yb, x, bc, sin, cols, gate, gg, skip, gain, gated, gscan, ggate, ggain, go, sel, ys, ws, gw, acc):
    i = pl.program_id(0)
    half = ya.shape[1]
    di = 2 * half

    @pl.when(i == 0)
    def _():
        for g in range(ng):
            sel[:, g * GW : (g + 1) * GW] = pick(8 * g, GW, hd)
        ggain[...] = jnp.zeros_like(ggain)
        acc[...] = jnp.zeros_like(acc)

    for g in range(ng):
        k = slice(g * GW, (g + 1) * GW)
        w = mm(cols[0], sel[:, k]) + mm(cols[1], sel[:, k])
        ws[:, k] = w
        ys[:, k] = mm(bc[:, 128:256], sin[g]) * w
    inv_di = 1.0 / di

    def body(q, carry):
        r = pl.ds(pl.multiple_of(q * SR, SR), SR)
        local = jnp.concatenate([ya[r, :], yb[r, :]], 1)
        y = local + ys[r, :] + skip[0:1] * x[r, :].astype(f32)
        scanned = y.astype(bf16).astype(f32)
        gt = gate[r, :].astype(f32)
        sg = sigmoid(gt)
        sil = gt * sg
        v = scanned * sil
        ginv = lax.rsqrt(jnp.sum(v * v, 1, keepdims=True) * inv_di + epsilon)
        vn = v * ginv
        gated[r, :] = (vn * gain[0:1]).astype(bf16)
        grad = gg[r, :]
        part = grad * vn
        ggain[0:8] += part[0:8] + part[8:16]
        gl = gain[0:1] * grad
        mean = jnp.sum(gl * v, 1, keepdims=True) * inv_di
        gv = ginv * (gl - v * (ginv * ginv * mean))
        gs = (gv * sil).astype(bf16)
        gscan[r, :] = gs
        ggate[r, :] = (gv * scanned * (sg * (1.0 + gt * (1.0 - sg)))).astype(bf16)
        gw[r, :] = (gs.astype(f32) * ws[r, :]).astype(bf16)
        return carry

    lax.fori_loop(0, LB // SR, body, 0)
    for g in range(ng):
        k = slice(g * GW, (g + 1) * GW)
        acc[g] += mm_tn(bc[:, 128:256], gw[:, k])

    @pl.when(i == pl.num_programs(0) - 1)
    def _():
        go[...] = acc[...].astype(bf16)


def call_c(ya, yb, x, bc, sin, cols, gate, gg, skip, gain, rows, di, hd):
    ng = di // GW
    row = lambda i: (i, 0)
    full = lambda i: (0, 0)
    cube = lambda i: (0, 0, 0)
    wide = pl.BlockSpec((LB, di), row)
    return pl.pallas_call(
        functools.partial(kernel_c, ng, hd),
        grid=(rows // LB,),
        in_specs=[
            pl.BlockSpec((LB, di // 2), row),
            pl.BlockSpec((LB, di // 2), row),
            wide,
            pl.BlockSpec((LB, GW), row),
            pl.BlockSpec((ng, 128, GW), cube),
            pl.BlockSpec((2, LB, 128), lambda i: (0, i, 0)),
            wide,
            wide,
            pl.BlockSpec((8, di), full),
            pl.BlockSpec((8, di), full),
        ],
        out_specs=[wide, wide, wide, pl.BlockSpec((8, di), full), pl.BlockSpec((ng, 128, GW), cube)],
        out_shape=[
            jax.ShapeDtypeStruct((rows, di), bf16),
            jax.ShapeDtypeStruct((rows, di), bf16),
            jax.ShapeDtypeStruct((rows, di), bf16),
            jax.ShapeDtypeStruct((8, di), f32),
            jax.ShapeDtypeStruct((ng, 128, GW), bf16),
        ],
        scratch_shapes=[
            pltpu.VMEM((128, di), bf16),
            pltpu.VMEM((LB, di), f32),
            pltpu.VMEM((LB, di), f32),
            pltpu.VMEM((LB, di), bf16),
            pltpu.VMEM((ng, 128, GW), f32),
        ],
        compiler_params=pltpu.CompilerParams(dimension_semantics=("arbitrary",)),
        cost_estimate=pl.CostEstimate(flops=1200000000, bytes_accessed=20000000, transcendentals=2000000),
        name="gate_both",
    )(ya, yb, x, bc, sin, cols, gate, gg, skip, gain)


def kernel_d(rows, hd, x, dy, bc, cols, cumt, stept, stepall, masks, mrow, sin, gin, cin, cw, skip, dtt, hp,
             gci, tail, rim, gcw, gdt, hsum,
             score, neg, cumb, stepb, states, zsum, gact, dbc, ext, shifted, arow, crow, grow, xrow, adj):
    i = pl.program_id(0)
    n = rows // LB
    last = pl.num_programs(0) - 1

    @pl.when(i == 0)
    def _():
        for c in range(n):
            r = slice(c * LB, (c + 1) * LB)
            score[c] = mm_nt(bc[r, 0:128], bc[r, 128:256])
            neg[c] = negmask(masks, mrow, c, True)
        zsum[...] = jnp.zeros_like(zsum)
        dbc[...] = jnp.zeros_like(dbc)
        zero = jnp.zeros((8, GW), f32)
        for k in range(TAPS):
            shifted[k, 0:8] = zero
            shifted[k, rows + 8 : rows + 16] = zero

    @pl.when(i < last)
    def _():
        g = i
        sel = pick(8 * g, 4 * LB, LB)
        cumb[...] = mm(cols[0], sel) + mm(cols[1], sel) + mm(cols[2], sel)
        sel = pick(64 + 8 * g, 4 * LB, LB)
        stepb[...] = mm(cols[0], sel) + mm(cols[1], sel) + mm(cols[2], sel)
        sel0 = pick(8 * g, GW, hd)
        sel64 = pick(64 + 8 * g, GW, hd)
        heads = head_rows(hd)
        low, high = half_masks(hd)
        lane = lax.broadcasted_iota(jnp.int32, (LB, 128), 1)
        states[0] = sin[0]
        run = sin[0].astype(f32)
        for c in range(n - 1):
            r = slice(c * LB, (c + 1) * LB)
            e = slice((c + 1) * LB - 16, (c + 1) * LB)
            dec = (mm(cols[3, e], sel0) + mm(cols[4, e], sel0))[15:16]
            w_es = mm(cols[5, r], sel0) + mm(cols[6, r], sel0)
            run = run * dec + mm_tn(bc[r, 0:128], (x[r].astype(f32) * w_es).astype(bf16))
            states[c + 1] = run.astype(bf16)
        adj[...] = gin[0].astype(f32)
        slot = pl.ds(pl.multiple_of(8 * g, 8), 8)
        skipsum = jnp.zeros((1, GW), f32)
        for c in reversed(range(n)):
            r = slice(c * LB, (c + 1) * LB)
            xf = x[r].astype(f32)
            dyf = dy[r].astype(f32)
            b_c, c_c = bc[r, 0:128], bc[r, 128:256]
            w_in = mm(cols[3, r], sel0) + mm(cols[4, r], sel0)
            w_end = mm(cols[3, r], sel64) + mm(cols[4, r], sel64)
            w_es = mm(cols[5, r], sel0) + mm(cols[6, r], sel0)
            st_e = mm(cols[0, r], sel64) + mm(cols[1, r], sel64)
            big = adj[...]
            adj_b = big.astype(bf16)
            st_b = states[c]
            du_out = mm(b_c, adj_b) * w_end
            dbc[r, 0:128] += mm_nt((xf * w_es).astype(bf16), adj_b)
            dyw = dyf * w_in
            dyw_b = dyw.astype(bf16)
            dbc[r, 128:256] += mm_nt(dyw_b, st_b)
            from_state = lane_sums(heads, dyw * mm(c_c, st_b))
            dec = w_in[LB - 1 : LB]
            cross = jnp.sum(big * st_b.astype(f32), 0, keepdims=True) * dec
            cross = lane_sums(heads, jnp.broadcast_to(cross, (LB, GW)))
            adj[...] = big * dec + mm_tn(c_c, dyw_b)
            x_out = lane_sums(heads, xf * du_out)
            zacc = zsum[c]
            pcol = jnp.zeros((LB, 128), f32)
            rsum = []
            dus = []
            for p in range(2):
                k = slice(128 * p, 128 * (p + 1))
                xp, dyp = x[r, k], dy[r, k]
                both = mm_nt(jnp.concatenate([xp * low, xp * high], 0), dyp)
                mats = []
                for j in range(2):
                    h = 2 * p + j
                    hb = slice(h * LB, (h + 1) * LB)
                    diff = cumt[h : h + 1, r] - cumb[r, hb]
                    dmat = jnp.exp(diff + neg[c])
                    kmat = dmat * both[j * LB : (j + 1) * LB]
                    kq = kmat * score[c]
                    sb = stepb[r, hb]
                    zacc = zacc + kmat * sb
                    pcol = jnp.where(lane == h, jnp.sum(kq, 1, keepdims=True), pcol)
                    rsum.append(jnp.sum(kq * sb, 0, keepdims=True))
                    mats.append((dmat * score[c]).astype(bf16))
                dus.append(mm(jnp.concatenate(mats, 1), jnp.concatenate([dyp * low, dyp * high], 0)))
            zsum[c] = zacc
            p_t = pcol.T[0:8]
            rsum = jnp.concatenate(rsum + [jnp.zeros((4, LB), f32)], 0)
            arow[slot, r] = rsum - stept[:, r] * p_t + from_state
            crow[slot, r] = stept[:, r] * x_out
            grow[slot, r] = cross
            xrow[slot, r] = p_t + x_out
            du = jnp.concatenate(dus, 1) + du_out
            gx = st_e * du + skip[0:1] * dyf
            gact[r] = gx.astype(bf16).astype(f32)
            skipsum = skipsum + jnp.sum(xf * dyf, 0, keepdims=True)
        gcw[TAPS + 1 : TAPS + 2] = skipsum

    @pl.when(i == last)
    def _():
        for c in range(n):
            r = slice(c * LB, (c + 1) * LB)
            z = zsum[c].astype(bf16)
            gact[r, 0:128] = dbc[r, 0:128] + mm(z, bc[r, 128:256])
            gact[r, 128:256] = dbc[r, 128:256] + mm_tn(z, bc[r, 0:128])
        rate = jnp.exp(hp[:, 1:2])
        sums = jnp.zeros((64, 1), f32)
        alog = jnp.zeros((64, 1), f32)
        for c in range(n):
            r = slice(c * LB, (c + 1) * LB)
            cr = crow[:, r]
            gl = scan_lanes(arow[:, r], True) + scan_lanes(cr, False) - cr + grow[:, r]
            grad = (xrow[:, r] - rate * gl) * sigmoid(dtt[:, r] + hp[:, 0:1])
            gdt[:, r] = grad
            sums = sums + jnp.sum(grad, 1, keepdims=True)
            alog = alog - jnp.sum(gl * (rate * stepall[:, r]), 1, keepdims=True)
        lane = lax.broadcasted_iota(jnp.int32, (64, 128), 1)
        hsum[...] = jnp.where(lane == 0, sums, jnp.where(lane == 1, alog, 0.0))
        gcw[TAPS + 1 : TAPS + 2] = jnp.zeros((1, GW), f32)

    fill_extended(ext, cin, rows)
    parts = [jnp.zeros((8, GW), f32) for _ in range(TAPS + 1)]
    for r in range(0, rows, RC):
        pre = conv_pre(ext, cw, masks, r)
        s = sigmoid(pre)
        gp = gact[r : r + RC] * (s * (1.0 + pre * (1.0 - s)))
        for k in range(TAPS):
            gm = gp if k == TAPS - 1 else gp * masks[r : r + RC, k : k + 1]
            shifted[k, 8 + r : 8 + r + RC] = gm
            off = 8 - (TAPS - 1) + k + r
            prod = gm * ext[off : off + RC]
            for q in range(0, RC, 8):
                parts[k] = parts[k] + prod[q : q + 8]
        for q in range(0, RC, 8):
            parts[TAPS] = parts[TAPS] + gp[q : q + 8]
    for k in range(TAPS + 1):
        gcw[k : k + 1] = jnp.sum(parts[k], 0, keepdims=True)

    def back(start, count):
        total = None
        for k in range(TAPS):
            off = start + TAPS - 1 - k
            term = shifted[k, off : off + count] * cw[k : k + 1]
            total = term if total is None else total + term
        return total

    rim[...] = back(0, 8)
    for r in range(0, rows, RC):
        value = back(8 + r, RC)
        gci[r : r + RC] = value.astype(bf16)
        if r == rows - RC:
            tail[...] = value[RC - HALO : RC]


def call_d(x, dy, bc, cols, cumt, stept, masks, mrow, sin, gin, pc, cw, skip, dtt, hp, rows, di, hd):
    ng = di // GW
    n = rows // LB
    ch = di + GW
    own = lambda i: (0, jnp.minimum(i, ng - 1))
    row = lambda i: (jnp.minimum(i, ng - 1), 0)
    cube = lambda i: (jnp.minimum(i, ng - 1), 0, 0)
    blk = lambda i: (0, i)
    full = lambda i: (0, 0)
    return pl.pallas_call(
        functools.partial(kernel_d, rows, hd),
        grid=(ng + 1,),
        in_specs=[
            pl.BlockSpec((rows, GW), own),
            pl.BlockSpec((rows, GW), own),
            pl.BlockSpec((rows, GW), full),
            pl.BlockSpec((9, rows, 128), lambda i: (0, 0, 0)),
            pl.BlockSpec((8, rows), row),
            pl.BlockSpec((8, rows), row),
            pl.BlockSpec((64, rows), full),
            pl.BlockSpec((rows, 8), full),
            pl.BlockSpec((8, rows), full),
            pl.BlockSpec((1, 128, GW), cube),
            pl.BlockSpec((1, 128, GW), cube),
            pl.BlockSpec((rows + HALO, GW), blk),
            pl.BlockSpec((8, GW), blk),
            pl.BlockSpec((8, GW), own),
            pl.BlockSpec((64, rows), full),
            pl.BlockSpec((64, 8), full),
        ],
        out_specs=[
            pl.BlockSpec((rows, GW), blk),
            pl.BlockSpec((HALO, GW), blk),
            pl.BlockSpec((8, GW), blk),
            pl.BlockSpec((8, GW), blk),
            pl.BlockSpec((64, rows), full),
            pl.BlockSpec((64, 128), full),
        ],
        out_shape=[
            jax.ShapeDtypeStruct((rows, ch), bf16),
            jax.ShapeDtypeStruct((HALO, ch), f32),
            jax.ShapeDtypeStruct((8, ch), f32),
            jax.ShapeDtypeStruct((8, ch), f32),
            jax.ShapeDtypeStruct((64, rows), f32),
            jax.ShapeDtypeStruct((64, 128), f32),
        ],
        scratch_shapes=[
            pltpu.VMEM((n, LB, LB), f32),
            pltpu.VMEM((n, LB, LB), f32),
            pltpu.VMEM((rows, 4 * LB), f32),
            pltpu.VMEM((rows, 4 * LB), f32),
            pltpu.VMEM((n, 128, GW), bf16),
            pltpu.VMEM((n, LB, LB), f32),
            pltpu.VMEM((rows, GW), f32),
            pltpu.VMEM((rows, GW), f32),
            pltpu.VMEM((rows + 8, GW), f32),
            pltpu.VMEM((TAPS, rows + 16, GW), f32),
            pltpu.VMEM((64, rows), f32),
            pltpu.VMEM((64, rows), f32),
            pltpu.VMEM((64, rows), f32),
            pltpu.VMEM((64, rows), f32),
            pltpu.VMEM((128, GW), f32),
        ],
        compiler_params=pltpu.CompilerParams(dimension_semantics=("arbitrary",)),
        cost_estimate=pl.CostEstimate(flops=4000000000, bytes_accessed=14000000, transcendentals=4000000),
        name="scan_backward",
    )(x, dy, bc, cols, cumt, stept, stept, masks, mrow, sin, gin, pc, cw, skip, dtt, hp)


def slots(values, per):
    groups = values.shape[0] // per
    shaped = values.reshape((groups, per) + values.shape[1:])
    pad = [(0, 0), (0, 8 - per)] + [(0, 0)] * (values.ndim - 1)
    return jnp.pad(shaped, pad).reshape((groups * 8,) + values.shape[1:])


def unslots(values, per):
    groups = values.shape[0] // 8
    return values.reshape((groups, 8) + values.shape[1:])[:, :per].reshape((groups * per,) + values.shape[1:])


def gather_small(value, axis):
    count = lax.axis_size(axis)
    wide = jnp.broadcast_to(value[None], (count,) + value.shape)
    return lax.all_to_all(wide, axis, split_axis=0, concat_axis=0, tiled=True)


def gather_weight(shard):
    part = shard.shape[0] // lax.axis_size("seq")
    mine = lax.dynamic_slice_in_dim(shard, lax.axis_index("seq") * part, part)
    return lax.all_gather(mine, ("wsh", "seq"), axis=0, tiled=True)


def reduce_weight(grad):
    part = lax.psum_scatter(grad, "seq", scatter_dimension=0, tiled=True)
    part = lax.psum_scatter(part, "wsh", scatter_dimension=0, tiled=True)
    return lax.all_gather(part, "seq", axis=0, tiled=True)


def local(x_in, seg_ids, in_weight, out_weight, conv_weight, conv_bias, dt_bias, a_log, skip_gain, norm_gain, gate_gain, cotangent):
    nseq, nw = lax.axis_size("seq"), lax.axis_size("wsh")
    me = lax.axis_index("seq")
    rows, d = x_in.shape[1:]
    e = in_weight.shape[1]
    di = out_weight.shape[0] * nw
    heads = dt_bias.shape[0] * nw
    ch = conv_bias.shape[0] * nw
    hd = di // heads
    per = GW // hd
    ng = di // GW
    x, ids, cot = x_in[0], seg_ids[0], cotangent[0]

    forward = [(i, i + 1) for i in range(nseq - 1)]
    x_halo = lax.ppermute(x[rows - HALO :], "seq", forward)
    id_halo = lax.ppermute(ids[rows - HALO :], "seq", forward)
    id_halo = jnp.where(me == 0, -1, id_halo)

    w_cd = gather_weight(in_weight[:, di:])
    w_gate = gather_weight(in_weight[:, :di])
    w_out = gather_weight(out_weight)
    small = [conv_weight.reshape(-1), conv_bias, dt_bias, a_log, skip_gain, norm_gain, gate_gain]
    sizes = [s.shape[0] for s in small]
    packed = gather_small(jnp.concatenate(small), "wsh")
    cut, at = [], 0
    for s in sizes:
        cut.append(packed[:, at : at + s].astype(f32))
        at += s
    conv_w = cut[0].reshape(nw, TAPS, -1).transpose(1, 0, 2).reshape(TAPS, ch)
    conv_b, dtb, alog, skip_g, norm_g, gate_g = [c.reshape(-1) for c in cut[1:]]
    cw = jnp.concatenate([conv_w, conv_b[None], jnp.zeros((3, ch), f32)], 0)
    hp = jnp.pad(jnp.stack([slots(dtb, per), slots(alog, per)], 1), ((0, 0), (0, 6)))
    skip = jnp.broadcast_to(jnp.repeat(skip_g, hd)[None], (8, di))
    gain = jnp.broadcast_to(gate_g[None], (8, di))

    ext_ids = jnp.concatenate([id_halo[HALO - 3 :], ids])
    prev = id_halo[HALO - 1]
    before = jnp.repeat(jnp.concatenate([prev[None], ids[LB - 1 :: LB][:-1]]), LB)
    ends = jnp.repeat(ids[LB - 1 :: LB], LB)
    zero = jnp.zeros((rows,), f32)
    masks = jnp.stack([(ext_ids[k : k + rows] == ids).astype(f32) for k in range(3)] + [ids.astype(f32)] + [zero] * 4, 1)
    mrow = jnp.stack(
        [(ids == before).astype(f32), (ids == ends).astype(f32), (ids == prev).astype(f32), (ids == ids[rows - 1]).astype(f32), ids.astype(f32)]
        + [zero] * 3,
        0,
    )

    xf = jnp.concatenate([x, x_halo], 0).astype(f32)
    rinv = lax.rsqrt(jnp.mean(xf * xf, 1, keepdims=True) + epsilon)
    normed = (xf * rinv * norm_g[None]).astype(bf16)
    pc = mm(normed, w_cd).astype(bf16)
    normed_own = normed[:rows]
    dtt = slots(pc[:rows, ch:].T.astype(f32), per)

    xp, bc, s_loc, cumt, stept, cols = call_a(pc, cw, masks, mrow, dtt, hp, rows, di, hd)
    recv = lax.all_to_all(s_loc, "seq", split_axis=0, concat_axis=0, tiled=True)
    ya = call_b(xp, bc, cols, cumt, stept, masks, mrow, rows, hd, 0, ng // 2)
    s_all, dec = call_f(recv)
    s_in = lax.all_to_all(s_all, "seq", split_axis=0, concat_axis=0, tiled=True)
    yb = call_b(xp, bc, cols, cumt, stept, masks, mrow, rows, hd, ng // 2, ng - ng // 2)

    gate = mm(normed_own, w_gate).astype(bf16)
    gg = mm_nt(cot, w_out)
    gated, gscan, ggate, ggain, g_loc = call_c(ya, yb, xp, bc, s_in, cols[7:9], gate, gg, skip, gain, rows, di, hd)
    g_recv = lax.all_to_all(g_loc, "seq", split_axis=0, concat_axis=0, tiled=True)
    g_all = call_g(g_recv, dec)
    g_in = lax.all_to_all(g_all, "seq", split_axis=0, concat_axis=0, tiled=True)

    output = (x.astype(f32) + mm(gated, w_out)).astype(bf16)

    def ordered(values):
        r = values.shape[0] // (nw * nseq)
        return values.reshape(nw, nseq, r, values.shape[1]).transpose(1, 0, 2, 3).reshape(values.shape)

    r = d // (nw * nseq)
    normed_t = normed_own.reshape(rows, nw, nseq, r).transpose(0, 2, 1, 3).reshape(rows, d)
    grad_wout = reduce_weight(ordered(mm_tn(gated, cot).astype(bf16)))
    grad_wgate = reduce_weight(mm_tn(normed_t, ggate).astype(bf16))
    gn_gate = mm_nt(ggate, w_gate)

    gci, tail, rim, gcw, gdt, hsum = call_d(
        xp, gscan, bc, cols, cumt, stept, masks, mrow, s_in, g_in, pc, cw, skip, dtt, hp, rows, di, hd
    )
    backward = [(i + 1, i) for i in range(nseq - 1)]
    rim_next = lax.ppermute(rim[8 - (TAPS - 1) :], "seq", backward)
    fixed = jnp.concatenate([tail[: HALO - (TAPS - 1)], tail[HALO - (TAPS - 1) :] + rim_next], 0)
    gci = lax.dynamic_update_slice(gci, fixed.astype(bf16), (rows - HALO, 0))
    gcd = jnp.concatenate([gci, unslots(gdt, per).T.astype(bf16)], 1)
    grad_wcd = reduce_weight(mm_tn(normed_t, gcd).astype(bf16))
    gnorm = gn_gate + mm_nt(gcd, w_cd)
    x_own, rinv_own = xf[:rows], rinv[:rows]
    grad_norm = jnp.sum(gnorm * x_own * rinv_own, 0)
    gl = gnorm * norm_g[None]
    mean = jnp.mean(gl * x_own, 1, keepdims=True)
    grad_input = cot.astype(f32) + rinv_own * (gl - x_own * (rinv_own * rinv_own * mean))

    pieces = [
        gcw[:TAPS].reshape(TAPS, nw, -1).transpose(1, 0, 2).reshape(nw, -1),
        gcw[TAPS].reshape(nw, -1),
        unslots(hsum[:, 0], per).reshape(nw, -1),
        unslots(hsum[:, 1], per).reshape(nw, -1),
        jnp.sum(gcw[TAPS + 1, :di].reshape(heads, hd), 1).reshape(nw, -1),
        grad_norm.reshape(nw, -1),
        jnp.sum(ggain, 0).reshape(nw, -1),
    ]
    stacked = lax.all_to_all(jnp.concatenate(pieces, 1), "wsh", split_axis=0, concat_axis=0, tiled=True)
    total = jnp.sum(gather_small(jnp.sum(stacked, 0), "seq"), 0)
    outs, at = [], 0
    for s in sizes:
        outs.append(total[at : at + s])
        at += s
    return (
        output[None],
        grad_input[None],
        jnp.concatenate([grad_wgate, grad_wcd], 1).astype(f32),
        grad_wout.astype(f32),
        outs[0].reshape(TAPS, -1),
        outs[1],
        outs[2],
        outs[3],
        outs[4],
        outs[5],
        outs[6],
    )


def solution(mesh):
    act, wide, vec = P("wsh", "seq", None), P("wsh", None), P("wsh")
    in_specs = (act, P("wsh", "seq"), wide, wide, P(None, "wsh"), vec, vec, vec, vec, vec, vec, act)
    out_specs = (act, act, wide, wide, P(None, "wsh"), vec, vec, vec, vec, vec, vec)
    return jax.shard_map(local, mesh=mesh, in_specs=in_specs, out_specs=out_specs, check_vma=False)
```

time: 1670 us -> 600 us (0.36)
  waiting for transfers between devices: 658 us -> 298 us
  matrix products: 320 us -> 55.6 us
  local copies, waits for them, and re-layouts: 300 us -> 42.1 us
  other arithmetic: 211 us -> 20.5 us
  Pallas kernels: 0 us -> 103 us
  blocking collectives: 118 us -> 31.1 us
    reduce_scatter x3 -> x5, waiting for transfers between devices: 382 us -> 61.3 us  [the longest x3 61.2 us: reduce_weight(): part = lax.psum_scatter(part, 'wsh', scatter_dimension=0, tiled=True)]
    dot_general x118 -> x9, matrix products: 320 us -> 55.6 us  [the longest x3 21.8 us: mm_nt(): lax.dot_general(a, b, (((1,), (1,)), ((), ())), preferred_element_type=f32)]
    pallas_call x0 -> x7, Pallas kernels: none -> 103 us  [the longest x1 50.4 us: call_d(): pl.pallas_call(functools.partial(kernel_d, rows, hd), grid=(ng + 1,), in_...]
    dynamic_update_slice x26 -> x0, local copies, waits for them, and re-layouts: 102 us -> none  [the longest x24 101 us: scan_heads(): ignored, outputs = lax.scan(jax.checkpoint(one_block), initial, pieces)]
    another operation x68 -> x4, other arithmetic: 90.9 us -> 1 us
    all_to_all x6 -> x5, waiting for transfers between devices: 95.3 us -> 7.73 us  [the longest x1 5.68 us: local(): lax.all_to_all(jnp.concatenate(pieces, 1), 'wsh', split_axis=0, concat_ax...]
    psum x1 -> x0, waiting for transfers between devices: 71.6 us -> none  [local(): lax.psum((grad_win, grad_wout, grad_convw, grad_convb, grad_dtb, grad_alo...]
    all_gather x4 -> x0, blocking collectives: 65.4 us -> none  [the longest x1 31.8 us: local(): lax.all_gather(conv_weight, 'wsh', axis=1, tiled=True)]
  transfers between devices with their start and end apart: 16 -> 20, of which waited for: 8 -> 11; matrix products, arithmetic and copies ran while one was open for 25% -> 16% of each run, Pallas kernels for 0% -> 15%
where the time goes in v1:
time: 600 us; the launch traced here: 593 us
  waiting for transfers between devices  298 us (50%)
  Pallas kernels  103 us (17%)
  matrix products  55.6 us (9%)
  local copies, waits for them, and re-layouts  42.1 us (7%)
  blocking collectives  31.1 us (5%)
  starting transfers between devices  27.8 us (5%)
  other arithmetic  20.5 us (3%)
  between operations  15.2 us (3%)
    all_gather x3, waiting for transfers between devices, gather_weight(): return lax.all_gather(mine, ('wsh', 'seq'), axis=0, tiled=True)  138 us
    reduce_scatter x3, waiting for transfers between devices, reduce_weight(): part = lax.psum_scatter(part, 'wsh', scatter_dimension=0, tiled=True)  61.2 us
    unnamed x13, waiting for transfers between devices  58.4 us
    pallas_call x1, Pallas kernels, call_d(): pl.pallas_call(functools.partial(kernel_d, rows, hd), grid=(ng + 1,), in_...  50.4 us
    all_gather x3, waiting for transfers between devices, reduce_weight(): return lax.all_gather(part, 'seq', axis=0, tiled=True)  32.8 us
    dot_general x3, matrix products, mm_nt(): lax.dot_general(a, b, (((1,), (1,)), ((), ())), preferred_element_type=f32)  21.8 us
    unnamed x49, local copies, waits for them, and re-layouts  19.3 us
    pallas_call x2, Pallas kernels, call_b(): pl.pallas_call(functools.partial(kernel_b, rows, hd, g0), grid=(count,),...  19.3 us
  transfers between devices with their start and end apart: 20, of which 11 were waited for; matrix products, arithmetic and copies ran while one was open for 16% of the time, Pallas kernels for 15%

profile of v1, /device:TPU:0, one launch (start us, length us, event | category | flops | bytes accessed | tf_op | source)
XLA Modules:
  0.0 592.7 jit_solution(655339472303289208)
XLA Ops:
  7.3 1.5 slice-done
  10.1 1.4 slice.158
  13.4 2.4 collective-permute-start.1
  18.1 5.7 all-to-all-start
  23.8 3.4 collective-permute-start
  29.6 1.3 compare_convert_fusion
  35.9 42.9 %all-gather.7.cloned.1.call-done = bf16[1024,2336]{1,0:T(8,128)(2,1)} async-done(((bf16[32,2336]{1,0:T(8,128)(2,1)}), bf16[1024,2336]{1,0:T(8,128)(2,1)}) %all-gather.7.cloned.1.call-update) | async-done | bytes 4784144 | tf_op jit(solution)/shard_map/all_gather | solution.py:668
  78.8 5.6 convolution_convert_fusion.1.cin
  84.4 1.5 copy-done.12
  86.7 13.5 %conv_state.1 = (bf16[512,2048]{1,0:T(8,128)(2,1)}, bf16[512,256]{1,0:T(8,128)(2,1)}, bf16[8,144,256]{2,1,0:T(8,128)(2,1)}, f32[64,512]{1,0:T(8,128)}, f32[64,512]{1,0:T(8,128)}, /*index=5*/bf16[9,512,128]{2,1,0:T(8,128)(2,1)}) custom-call(bf16[528,2336]{1,0:T(8,128)(2,1)} %copy-done.12, f32[8,2304]{1,0:T(8,128)} %maximum_maximum_fusion.cw, ...), custom_call_target="tpu_custom_call" | custom-call | flops 400000000 | bytes 6000000 | tf_op jit(solution)/shard_map/conv_state/pallas_call | solution.py:159
  100.1 3.6 all-to-all-start.1
  103.7 41.1 %all-gather.9.cloned.1.call-done = bf16[1024,2048]{1,0:T(8,128)(2,1)} async-done(((bf16[32,2048]{1,0:T(8,128)(2,1)}), bf16[1024,2048]{1,0:T(8,128)(2,1)}) %all-gather.9.cloned.1.call-update) | async-done | bytes 4194320 | tf_op jit(solution)/shard_map/all_gather | solution.py:668
  144.8 5.8 convolution_convert_fusion.4.gate
  151.5 2.0 join_forward.1
  153.6 3.5 all-to-all-start.2
  157.3 53.5 %all-gather.11.cloned.1.call-done = bf16[2048,1024]{1,0:T(8,128)(2,1)} async-done(((bf16[64,1024]{1,0:T(8,128)(2,1)}), bf16[2048,1024]{1,0:T(8,128)(2,1)}) %all-gather.11.cloned.1.call-update) | async-done | bytes 4194320 | tf_op jit(solution)/shard_map/all_gather | solution.py:668
  210.8 6.9 %convolution_bitcast_fusion.gg = f32[512,2048]{1,0:T(8,128)} fusion(bf16[2048,1024]{1,0:T(8,128)(2,1)} %all-gather.11.cloned.1.call-done, bf16[1,512,1024]{2,1,0:T(8,128)(2,1)} %param.23), kind=kOutput, calls=%fused_computation.4 | convolution fusion | flops 2147483648 | bytes 9437184 | tf_op jit(solution)/shard_map/dot_general | solution.py:24
  217.7 1.7 slice.156.cols
  219.3 9.6 %scan_forward.3.yb = f32[512,1024]{1,0:T(8,128)} custom-call(bf16[512,2048]{1,0:T(8,128)(2,1)} %get-tuple-element.30.x, bf16[512,256]{1,0:T(8,128)(2,1)} %get-tuple-element.31.bc, bf16[9,512,128]{2,1,0:T(8,128)(2,1)} %get-tuple-element.32.cols, f32[64,512]{1,0:T(8,128)} %get-tuple-element.33.cumt, f32[64,512]{1,0:T(8,128)} %get-tuple-element.34.stept.stepall, ...), custom_call_target="tpu_custom_call" | custom-call | flops 800000000 | bytes 4000000 | tf_op jit(solution)/shard_map/scan_forward/pallas_call | solution.py:296
  229.0 9.6 %scan_forward.2.ya = f32[512,1024]{1,0:T(8,128)} custom-call(bf16[512,2048]{1,0:T(8,128)(2,1)} %get-tuple-element.30.x, bf16[512,256]{1,0:T(8,128)(2,1)} %get-tuple-element.31.bc, bf16[9,512,128]{2,1,0:T(8,128)(2,1)} %get-tuple-element.32.cols, f32[64,512]{1,0:T(8,128)} %get-tuple-element.33.cumt, f32[64,512]{1,0:T(8,128)} %get-tuple-element.34.stept.stepall, ...), custom_call_target="tpu_custom_call" | custom-call | flops 800000000 | bytes 4000000 | tf_op jit(solution)/shard_map/scan_forward/pallas_call | solution.py:296
  239.9 15.3 %gate_both.1 = (bf16[512,2048]{1,0:T(8,128)(2,1)}, bf16[512,2048]{1,0:T(8,128)(2,1)}, bf16[512,2048]{1,0:T(8,128)(2,1)}, f32[8,2048]{1,0:T(8,128)}, bf16[8,128,256]{2,1,0:T(8,128)(2,1)}) custom-call(f32[512,1024]{1,0:T(8,128)} %scan_forward.2.ya, f32[512,1024]{1,0:T(8,128)} %scan_forward.3.yb, bf16[512,2048]{1,0:T(8,128)(2,1)} %get-tuple-element.30.x, ...), custom_call_target="tpu_custom_call" | custom-call | flops 1200000000 | bytes 20000000 | tf_op jit(solution)/shard_map/gate_both/pallas_call | solution.py:384
  255.2 4.2 convolution_convert_fusion.2
  259.5 2.5 copy.114
  262.8 5.9 %convolution_convert_fusion.3 = bf16[1024,2048]{1,0:T(8,128)(2,1)} fusion(bf16[512,1024]{0,1:T(8,128)(2,1)S(1)} %bitcast.84, bf16[512,2048]{1,0:T(8,128)(2,1)} %get-tuple-element.38), kind=kOutput, calls=%fused_computation.3 | convolution fusion | flops 2149580800 | bytes 7340032 | tf_op jit(solution)/shard_map/dot_general | solution.py:28
  269.8 12.8 %all_to_all.44.recv = bf16[8,128,256]{2,1,0:T(8,128)(2,1)} all-to-all(bf16[8,128,256]{2,1,0:T(8,128)(2,1)S(1)} %copy-done.7), channel_id=1, replica_groups=mesh['seq'=8,'wsh'=4] {'seq'}, dimensions={0} | all-to-all | bytes 1048576 | tf_op jit(solution)/shard_map/all_to_all | solution.py:741
  282.6 2.1 join_backward.1
  284.7 18.3 %all_to_all.45.gin = bf16[8,128,256]{2,1,0:T(8,128)(2,1)} all-to-all(bf16[8,128,256]{2,1,0:T(8,128)(2,1)} %join_backward.1), channel_id=1, replica_groups=mesh['seq'=8,'wsh'=4] {'seq'}, dimensions={0} | all-to-all | bytes 1048576 | tf_op jit(solution)/shard_map/all_to_all | solution.py:743
  303.1 50.4 %scan_backward.1 = (bf16[512,2304]{1,0:T(8,128)(2,1)}, f32[16,2304]{1,0:T(8,128)}, f32[8,2304]{1,0:T(8,128)}, f32[8,2304]{1,0:T(8,128)}, f32[64,512]{1,0:T(8,128)}, /*index=5*/f32[64,128]{1,0:T(8,128)}) custom-call(bf16[512,2048]{1,0:T(8,128)(2,1)} %get-tuple-element.30.x, bf16[512,2048]{1,0:T(8,128)(2,1)} %get-tuple-element.39.dy, ...), custom_call_target="tpu_custom_call" | custom-call | flops 4000000000 | bytes 14000000 | tf_op jit(solution)/shard_map/scan_backward/pallas_call | solution.py:587
  359.3 6.1 %convolution_convert_fusion = bf16[1024,2336]{0,1:T(8,128)(2,1)} fusion(bf16[512,1024]{0,1:T(8,128)(2,1)S(1)} %bitcast.85, bf16[512,32]{1,0:T(8,128)(2,1)S(1)} %bitcast.94, bf16[512,2304]{1,0:T(8,128)(2,1)} %maximum_dynamic-update-slice_fusion), kind=kOutput, calls=%fused_computation | convolution fusion | flops 2456649728 | bytes 8224768 | tf_op jit(solution)/shard_map/dot_general | solution.py:28
  365.3 7.4 %copy.120 = bf16[1024,2336]{1,0:T(8,128)(2,1)} copy(bf16[1024,2336]{0,1:T(8,128)(2,1)} %convolution_convert_fusion) | data formatting | bytes 9568256
  374.3 56.9 %reduce-scatter.19.cloned.1.call-done = bf16[128,2336]{1,0:T(8,128)(2,1)} async-done(((bf16[1024,2336]{1,0:T(8,128)(2,1)}), bf16[128,2336]{1,0:T(8,128)(2,1)}) %reduce-scatter.19.cloned.1.call-update) | async-done | bytes 598032
  431.3 24.1 %reduce-scatter.17.cloned.1.call-done = bf16[64,1024]{1,0:T(8,128)(2,1)} async-done(((bf16[256,1024]{1,0:T(8,128)(2,1)}), bf16[64,1024]{1,0:T(8,128)(2,1)}) %reduce-scatter.17.cloned.1.call-update) | async-done | bytes 131088 | tf_op jit(solution)/shard_map/reduce_scatter | solution.py:673
  455.4 22.4 %reduce-scatter.13.cloned.1.call-done = bf16[32,2048]{1,0:T(8,128)(2,1)} async-done(((bf16[128,2048]{1,0:T(8,128)(2,1)}), bf16[32,2048]{1,0:T(8,128)(2,1)}) %reduce-scatter.13.cloned.1.call-update) | async-done | bytes 131088 | tf_op jit(solution)/shard_map/reduce_scatter | solution.py:673
  478.1 1.6 maximum_convert_fusion.1
  479.7 6.1 %fusion.2 = bf16[1,512,1024]{2,1,0:T(8,128)(2,1)} fusion(bf16[512,2048]{1,0:T(8,128)(2,1)} %get-tuple-element.37, bf16[2048,1024]{1,0:T(8,128)(2,1)} %all-gather.11.cloned.1.call-done, bf16[1,512,1024]{2,1,0:T(8,128)(2,1)S(1)} %copy-done.2), kind=kOutput, calls=%fused_computation.16 | convolution fusion | flops 2149056512 | bytes 8388608 | tf_op jit(solution)/shard_map/dot_general | solution.py:20
  485.8 14.8 %reduce-scatter.21.cloned.1.call-done = bf16[32,2336]{1,0:T(8,128)(2,1)} async-done(((bf16[128,2336]{1,0:T(8,128)(2,1)}), bf16[32,2336]{1,0:T(8,128)(2,1)}) %reduce-scatter.21.cloned.1.call-update) | async-done | bytes 149520 | tf_op jit(solution)/shard_map/reduce_scatter | solution.py:673
  500.7 6.7 %fusion.13 = f32[512,1024]{1,0:T(8,128)} fusion(bf16[512,2048]{1,0:T(8,128)(2,1)} %get-tuple-element.38, bf16[1024,2048]{1,0:T(8,128)(2,1)} %all-gather.9.cloned.1.call-done), kind=kOutput, calls=%fused_computation.67 | convolution fusion | flops 2147483648 | bytes 8388608 | tf_op jit(solution)/shard_map/dot_general | solution.py:24
  508.5 8.3 %multiply_reduce_fusion.1 = (f32[1024]{0:T(1024)S(1)}, f32[512]{0:T(512)S(1)}, f32[512,1024]{1,0:T(8,128)}) fusion(f32[528,1024]{1,0:T(8,128)S(1)} %copy-done.3, f32[512]{0:T(512)S(1)} %slice.161, f32[1024]{0:T(1024)S(1)} %bitcast.97, f32[512,1024]{1,0:T(8,128)} %fusion.13, bf16[1024,2336]{1,0:T(8,128)(2,1)} %all-gather.7.cloned.1.call-done, ...), kind=kOutput, calls=%fused_computation.10 | convolution fusion | flops 2457926144 | bytes 13479936 | tf_op jit(solution)/shard_map/dot_general | solution.py:24
  517.6 3.3 all-to-all-start.5
  521.0 5.7 all-to-all-done.5
  527.4 3.8 all-to-all-start.6
  531.2 3.4 add_bitcast_fusion
  534.6 2.0 all-to-all-done.6
  539.9 2.8 convert_element_type.116
  542.7 6.8 %all-gather.13.cloned.1.call-done = bf16[256,2048]{1,0:T(8,128)(2,1)} async-done(((bf16[32,2048]{1,0:T(8,128)(2,1)}), bf16[256,2048]{1,0:T(8,128)(2,1)}) %all-gather.13.cloned.1.call-update) | async-done | bytes 1048592 | tf_op jit(solution)/shard_map/all_gather | solution.py:674
  549.5 26.0 %all-gather.15.cloned.1.call-done = bf16[256,2336]{1,0:T(8,128)(2,1)} async-done(((bf16[32,2336]{1,0:T(8,128)(2,1)}), bf16[256,2336]{1,0:T(8,128)(2,1)}) %all-gather.15.cloned.1.call-update) | async-done | bytes 1196048 | tf_op jit(solution)/shard_map/all_gather | solution.py:674
  575.5 4.0 maximum_convert_fusion
  579.5 5.9 %copy.118 = f32[256,4384]{0,1:T(8,128)} copy(f32[256,4384]{1,0:T(8,128)} %maximum_convert_fusion) | data formatting | bytes 8978432
  (183 shorter events, 31.3 us)
Async XLA Ops:
  7.2 5.4 copy-start
  7.2 1.6 slice-start
  7.2 71.6 %all-gather.7.cloned.1.call-start = ((), (), s32[]{:S(2)}) async-start(), calls=%async_computation.13 | async-start | bytes 5136384 | tf_op jit(solution)/shard_map/all_gather | solution.py:668
  9.9 3.4 copy-start.11
  9.9 5.9 copy-start.13
  9.9 5.9 %copy-start.14 = (bf16[576]{0:T(1024)(128)(2,1)S(1)}, bf16[576]{0:T(1024)(128)(2,1)}, u32[]{:S(2)}) copy-start(bf16[576]{0:T(1024)(128)(2,1)} %param.17) | copy-start | bytes 3460
  10.0 5.9 %copy-start.15 = (bf16[512]{0:T(512)(128)(2,1)S(1)}, bf16[512]{0:T(512)(128)(2,1)}, u32[]{:S(2)}) copy-start(bf16[512]{0:T(512)(128)(2,1)} %param.22) | copy-start | bytes 3076
  10.0 5.9 copy-start.16
  10.0 5.9 copy-start.17
  10.0 5.9 copy-start.18
  10.0 5.9 copy-start.19
  10.0 13.8 %copy-start.2 = (bf16[1,512,1024]{2,1,0:T(8,128)(2,1)S(1)}, bf16[1,512,1024]{2,1,0:T(8,128)(2,1)}, u32[]{:S(2)}) copy-start(bf16[1,512,1024]{2,1,0:T(8,128)(2,1)} %param.12) | copy-start | bytes 3145732
  10.0 134.8 %all-gather.9.cloned.1.call-start = ((), (), s32[]{:S(2)}) async-start(), calls=%async_computation.14 | async-start | bytes 4325376 | tf_op jit(solution)/shard_map/all_gather | solution.py:668
  12.6 198.2 %all-gather.11.cloned.1.call-start = ((), (), s32[]{:S(2)}) async-start(), calls=%async_computation.15 | async-start | bytes 4325376 | tf_op jit(solution)/shard_map/all_gather | solution.py:668
  13.4 14.6 %collective-permute-start.1 = (s32[16]{0:T(128)S(1)}, s32[16]{0:T(128)S(1)}, u32[]{:S(2)}, u32[]{:S(2)}) collective-permute-start(s32[16]{0:T(128)S(1)} %slice_bitcast_fusion.2), channel_id=1, source_target_pairs={{0,4},{4,8},{8,12},{12,16},{16,20},{20,24},{24,28},{1,5},{5,9},{9,... | collective-permute-start | bytes 200 | tf_op jit(solution)/shard_map/ppermute | solution.py:692
  18.1 14.7 %all-to-all-start = ((bf16[4,2,1836]{2,1,0:T(2,128)(2,1)}), bf16[4,2,1836]{2,1,0:T(2,128)(2,1)S(1)}, u32[]{:S(2)}, u32[]{:S(2)}) async-start(bf16[4,2,1836]{2,1,0:T(2,128)(2,1)} %reshape.215), calls=%async_computation | async-start | bytes 61440 | tf_op jit(solution)/shard_map/all_to_all | solution.py:662
  23.8 8.7 %collective-permute-start = (bf16[16,1024]{1,0:T(8,128)(2,1)S(1)}, bf16[16,1024]{1,0:T(8,128)(2,1)S(1)}, u32[]{:S(2)}, u32[]{:S(2)}) collective-permute-start(bf16[16,1024]{1,0:T(8,128)(2,1)S(1)} %slice_bitcast_fusion.1), channel_id=1, source_target_pairs={{0,4},{4,8},{8,12},{12,16},{16,20},{20,24},{24,28},{1,5},{5,9},{9,... | collective-permute-start | bytes 98312 | tf_op jit(solution)/shard_map/ppermute | solution.py:691
  84.4 1.5 copy-start.12
  100.1 50.6 %all-to-all-start.1 = ((bf16[8,144,256]{2,1,0:T(8,128)(2,1)}), bf16[8,144,256]{2,1,0:T(8,128)(2,1)S(1)}, u32[]{:S(2)}, u32[]{:S(2)}) async-start(bf16[8,144,256]{2,1,0:T(8,128)(2,1)} %get-tuple-element.35), calls=%async_computation.1 | async-start | bytes 1179648 | tf_op jit(solution)/shard_map/all_to_all | solution.py:732
  150.7 0.8 copy-start.4
  153.6 85.0 %all-to-all-start.2 = ((bf16[8,128,256]{2,1,0:T(8,128)(2,1)}), bf16[8,128,256]{2,1,0:T(8,128)(2,1)S(1)}, u32[]{:S(2)}, u32[]{:S(2)}) async-start(bf16[8,128,256]{2,1,0:T(8,128)(2,1)} %get-tuple-element.36), calls=%async_computation.2 | async-start | bytes 1048576 | tf_op jit(solution)/shard_map/all_to_all | solution.py:735
  157.1 215.7 %reduce-scatter.15.cloned.1.call-start = ((), (), s32[]{:S(2)}) async-start(), calls=%async_computation.20 | async-start | bytes 4718592 | tf_op jit(solution)/shard_map/reduce_scatter | solution.py:672
  238.6 1.3 copy-start.5
  262.1 111.5 %reduce-scatter.11.cloned.1.call-start = ((), (), s32[]{:S(2)}) async-start(), calls=%async_computation.16 | async-start | bytes 4718592 | tf_op jit(solution)/shard_map/reduce_scatter | solution.py:672
  268.8 1.1 copy-start.7
  268.8 162.4 %reduce-scatter.19.cloned.1.call-start = ((), (), s32[]{:S(2)}) async-start(), calls=%async_computation.23 | async-start | bytes 5603328
  354.4 3.3 collective-permute-start.2
  372.7 82.6 %reduce-scatter.17.cloned.1.call-start = ((), (), s32[]{:S(2)}) async-start(), calls=%async_computation.21 | async-start | bytes 655360 | tf_op jit(solution)/shard_map/reduce_scatter | solution.py:673
  373.5 104.3 %reduce-scatter.13.cloned.1.call-start = ((), (), s32[]{:S(2)}) async-start(), calls=%async_computation.17 | async-start | bytes 655360 | tf_op jit(solution)/shard_map/reduce_scatter | solution.py:673
  374.2 126.4 %reduce-scatter.21.cloned.1.call-start = ((), (), s32[]{:S(2)}) async-start(), calls=%async_computation.24 | async-start | bytes 778240 | tf_op jit(solution)/shard_map/reduce_scatter | solution.py:673
  431.2 108.7 %all-gather.17.cloned.1.call-start = ((), (), s32[]{:S(2)}) async-start(), calls=%async_computation.22 | async-start | bytes 1179648 | tf_op jit(solution)/shard_map/all_gather | solution.py:674
  455.4 94.2 %all-gather.13.cloned.1.call-start = ((), (), s32[]{:S(2)}) async-start(), calls=%async_computation.18 | async-start | bytes 1179648 | tf_op jit(solution)/shard_map/all_gather | solution.py:674
  477.8 97.7 %all-gather.15.cloned.1.call-start = ((), (), s32[]{:S(2)}) async-start(), calls=%async_computation.19 | async-start | bytes 1400832 | tf_op jit(solution)/shard_map/all_gather | solution.py:674
  500.6 6.7 %copy-start.9 = (f32[8,2048]{1,0:T(8,128)S(1)}, f32[8,2048]{1,0:T(8,128)}, u32[]{:S(2)}) copy-start(f32[8,2048]{1,0:T(8,128)} %get-tuple-element.48) | copy-start | bytes 196612
  500.7 6.7 %copy-start.10 = (f32[8,2304]{1,0:T(8,128)S(1)}, f32[8,2304]{1,0:T(8,128)}, u32[]{:S(2)}) copy-start(f32[8,2304]{1,0:T(8,128)} %get-tuple-element.46) | copy-start | bytes 221188
  500.7 7.4 %copy-start.8 = (f32[64,128]{1,0:T(8,128)S(1)}, f32[64,128]{1,0:T(8,128)}, u32[]{:S(2)}) copy-start(f32[64,128]{1,0:T(8,128)} %get-tuple-element.47) | copy-start | bytes 98308
  500.7 7.9 %copy-start.3 = (f32[528,1024]{1,0:T(8,128)S(1)}, f32[528,1024]{1,0:T(8,128)}, u32[]{:S(2)}) copy-start(f32[528,1024]{1,0:T(8,128)} %maximum_convert_fusion.1) | copy-start | bytes 6488068
  508.5 22.6 %copy-start.6 = (bf16[1,512,1024]{2,1,0:T(8,128)(2,1)S(1)}, bf16[1,512,1024]{2,1,0:T(8,128)(2,1)}, u32[]{:S(2)}) copy-start(bf16[1,512,1024]{2,1,0:T(8,128)(2,1)} %param.23) | copy-start | bytes 3145732
  517.6 9.0 %all-to-all-start.5 = ((f32[4,1,3672]{2,1,0:T(1,128)}), f32[4,1,3672]{2,1,0:T(1,128)S(1)}, u32[]{:S(2)}, u32[]{:S(2)}) async-start(f32[4,1,3672]{2,1,0:T(1,128)} %copy.116), calls=%async_computation.9 | async-start | bytes 118784 | tf_op jit(solution)/shard_map/all_to_all | solution.py:782
  527.4 9.3 %all-to-all-start.6 = ((f32[8,1,3672]{2,1,0:T(1,128)}), f32[8,1,3672]{2,1,0:T(1,128)S(1)}, u32[]{:S(2)}, u32[]{:S(2)}) async-start(f32[8,1,3672]{2,1,0:T(1,128)} %broadcast_in_dim.66), calls=%async_computation.10 | async-start | bytes 237568 | tf_op jit(solution)/shard_map/all_to_all | solution.py:662
  579.5 5.9 %copy-start.1 = (bf16[512,1024]{1,0:T(8,128)(2,1)S(1)}, bf16[512,1024]{1,0:T(8,128)(2,1)}, u32[]{:S(2)}) copy-start(bf16[512,1024]{1,0:T(8,128)(2,1)} %param.15) | copy-start | bytes 3145732
Sparse Core Ops, SparseCore 0:
  11.4 67.3 all-gather.6
  82.2 62.5 all-gather.8
  148.3 62.4 all-gather.10
  262.2 55.5 reduce-scatter.14
  321.5 51.1 reduce-scatter.10
  376.1 55.0 reduce-scatter.18
  433.5 21.8 reduce-scatter.16
  457.6 20.1 reduce-scatter.12
  480.1 20.5 reduce-scatter.20
  502.4 21.8 all-gather.16
  526.1 23.3 all-gather.12
  551.3 24.1 all-gather.14

commit v2 on v1

--- a/solution.py
+++ b/solution.py
@@ -94,9 +94,33 @@
     return pre
 
 
-def kernel_a(rows, hd, cin, cw, masks, mrow, dtt, hp, xo, bco, so, cumo, stepo, colo, ext, cols, act):
+def flat(w):
+    return w.reshape(w.shape[0] * w.shape[1], w.shape[2])
+
+
+def kernel_a(rows, hd, per, nq, me, nm, wx, wy, wb, cw, masks, mrow, hp, pxo, xo, bco, so, cumo, stepo, dto, colo, ext, cols, act):
     i = pl.program_id(0)
-    fill_extended(ext, cin, rows)
+
+    @pl.when(i == 0)
+    def _():
+        w = wb[...].reshape(wb.shape[0] * wb.shape[1], wb.shape[2])
+        out = mm(nm[...], w).astype(bf16)
+        pxo[...] = out[:, 0:GW]
+        dt = out[0:rows, GW : GW + 128].astype(f32).T
+        pieces = []
+        for g in range(8):
+            pieces += [dt[per * g : per * (g + 1)], jnp.zeros((8 - per, rows), f32)]
+        dto[...] = jnp.concatenate(pieces, 0)
+
+    @pl.when((i > 0) & (i <= nq))
+    def _():
+        pxo[...] = mm(nm[...], flat(wx[0])).astype(bf16)
+
+    @pl.when(i > nq)
+    def _():
+        pxo[...] = mm(nm[...], flat(wy[0])).astype(bf16)
+
+    fill_extended(ext, pxo, rows)
     for r in range(0, rows, RC):
         pre = conv_pre(ext, cw, masks, r)
         act[r : r + RC] = (pre * sigmoid(pre)).astype(bf16)
@@ -104,7 +128,7 @@
     @pl.when(i == 0)
     def _():
         bco[...] = act[...]
-        step = softplus(dtt[...] + hp[:, 0:1])
+        step = softplus(dto[...] + hp[:, 0:1])
         cum = scan_lanes(-jnp.exp(hp[:, 1:2]) * step, False)
         stepo[...] = step
         cumo[...] = cum
@@ -137,7 +161,7 @@
 
     @pl.when(i > 0)
     def _():
-        g = i - 1
+        g = block_of(i - 1, me, nq)
         x = act[...]
         xo[...] = x
         sel = pick(64 + 8 * g, GW, hd)
@@ -150,48 +174,64 @@
         so[0, 128:144] = jnp.concatenate([hi, lo, jnp.zeros((14, GW), bf16)], 0)
 
 
-def call_a(pc, cw, masks, mrow, dtt, hp, rows, di, hd):
+def block_of(j, me, nq):
+    return jnp.where(j < nq, me[1], 1 - me[1]) * nq + lax.rem(j, nq)
+
+
+def call_a(me, nm, wx, wy, wb, cw, masks, mrow, hp, rows, di, hd):
     ng = di // GW
     nb = ng + 1
-    col = lambda i: (0, (i + ng) % nb)
-    grp = lambda i: (0, jnp.maximum(i - 1, 0))
-    full = lambda i: (0, 0)
+    nq = wx.shape[0]
+    own = lambda i, me: block_of(jnp.maximum(i - 1, 0), me, nq)
+    col = lambda i, me: (0, jnp.where(i == 0, ng, own(i, me)))
+    grp = lambda i, me: (0, own(i, me))
+    full = lambda i, me: (0, 0)
+    cube = lambda i, me: (0, 0, 0)
     return pl.pallas_call(
-        functools.partial(kernel_a, rows, hd),
-        grid=(nb,),
-        in_specs=[
-            pl.BlockSpec((rows + HALO, GW), col),
-            pl.BlockSpec((8, GW), col),
-            pl.BlockSpec((rows, 8), full),
-            pl.BlockSpec((8, rows), full),
-            pl.BlockSpec((64, rows), full),
-            pl.BlockSpec((64, 8), full),
-        ],
-        out_specs=[
-            pl.BlockSpec((rows, GW), grp),
-            pl.BlockSpec((rows, GW), full),
-            pl.BlockSpec((1, 144, GW), lambda i: (jnp.maximum(i - 1, 0), 0, 0)),
-            pl.BlockSpec((64, rows), full),
-            pl.BlockSpec((64, rows), full),
-            pl.BlockSpec((9, rows, 128), lambda i: (0, 0, 0)),
-        ],
+        functools.partial(kernel_a, rows, hd, GW // hd, nq),
+        grid_spec=pltpu.PrefetchScalarGridSpec(
+            num_scalar_prefetch=1,
+            grid=(nb,),
+            in_specs=[
+                pl.BlockSpec(nm.shape, full),
+                pl.BlockSpec((1,) + wx.shape[1:], lambda i, me: (jnp.clip(i - 1, 0, nq - 1), 0, 0, 0)),
+                pl.BlockSpec((1,) + wx.shape[1:], lambda i, me: (jnp.clip(i - 1 - nq, 0, nq - 1), 0, 0, 0)),
+                pl.BlockSpec(wb.shape, cube),
+                pl.BlockSpec((8, GW), col),
+                pl.BlockSpec((rows, 8), full),
+                pl.BlockSpec((8, rows), full),
+                pl.BlockSpec((64, 8), full),
+            ],
+            out_specs=[
+                pl.BlockSpec((rows + HALO, GW), col),
+                pl.BlockSpec((rows, GW), grp),
+                pl.BlockSpec((rows, GW), full),
+                pl.BlockSpec((1, 144, GW), lambda i, me: (own(i, me), 0, 0)),
+                pl.BlockSpec((64, rows), full),
+                pl.BlockSpec((64, rows), full),
+                pl.BlockSpec((64, rows), full),
+                pl.BlockSpec((9, rows, 128), cube),
+            ],
+            scratch_shapes=[
+                pltpu.VMEM((rows + 8, GW), f32),
+                pltpu.VMEM((4, rows, 128), bf16),
+                pltpu.VMEM((rows, GW), bf16),
+            ],
+        ),
         out_shape=[
+            jax.ShapeDtypeStruct((rows + HALO, di + GW), bf16),
             jax.ShapeDtypeStruct((rows, di), bf16),
             jax.ShapeDtypeStruct((rows, GW), bf16),
             jax.ShapeDtypeStruct((ng, 144, GW), bf16),
             jax.ShapeDtypeStruct((64, rows), f32),
             jax.ShapeDtypeStruct((64, rows), f32),
+            jax.ShapeDtypeStruct((64, rows), f32),
             jax.ShapeDtypeStruct((9, rows, 128), bf16),
         ],
-        scratch_shapes=[
-            pltpu.VMEM((rows + 8, GW), f32),
-            pltpu.VMEM((4, rows, 128), bf16),
-            pltpu.VMEM((rows, GW), bf16),
-        ],
         compiler_params=pltpu.CompilerParams(dimension_semantics=("arbitrary",)),
-        cost_estimate=pl.CostEstimate(flops=400000000, bytes_accessed=6000000, transcendentals=2400000),
+        cost_estimate=pl.CostEstimate(flops=3000000000, bytes_accessed=12000000, transcendentals=2400000),
         name="conv_state",
-    )(pc, cw, masks, mrow, dtt, hp)
+    )(me, nm, wx, wy, wb, cw, masks, mrow, hp)
 
 
 def kernel_f(n, recv, sin, dec):
@@ -322,7 +362,7 @@
 SR = 16
 
 
-def kernel_c(ng, hd, ya, yb, x, bc, sin, cols, gate, gg, skip, gain, gated, gscan, ggate, ggain, go, sel, ys, ws, gw, acc):
+def kernel_c(ng, hd, ya, yb, x, bc, sin, whi, wlo, gate, gg, skip, gain, gated, gscan, ggate, ggain, go, sel, ys, ws, gw, acc):
     i = pl.program_id(0)
     half = ya.shape[1]
     di = 2 * half
@@ -336,7 +376,7 @@
 
     for g in range(ng):
         k = slice(g * GW, (g + 1) * GW)
-        w = mm(cols[0], sel[:, k]) + mm(cols[1], sel[:, k])
+        w = mm(whi[0], sel[:, k]) + mm(wlo[0], sel[:, k])
         ws[:, k] = w
         ys[:, k] = mm(bc[:, 128:256], sin[g]) * w
     inv_di = 1.0 / di
@@ -390,7 +430,8 @@
             wide,
             pl.BlockSpec((LB, GW), row),
             pl.BlockSpec((ng, 128, GW), cube),
-            pl.BlockSpec((2, LB, 128), lambda i: (0, i, 0)),
+            pl.BlockSpec((1, LB, 128), lambda i: (7, i, 0)),
+            pl.BlockSpec((1, LB, 128), lambda i: (8, i, 0)),
             wide,
             wide,
             pl.BlockSpec((8, di), full),
@@ -414,7 +455,7 @@
         compiler_params=pltpu.CompilerParams(dimension_semantics=("arbitrary",)),
         cost_estimate=pl.CostEstimate(flops=1200000000, bytes_accessed=20000000, transcendentals=2000000),
         name="gate_both",
-    )(ya, yb, x, bc, sin, cols, gate, gg, skip, gain)
+    )(ya, yb, x, bc, sin, cols, cols, gate, gg, skip, gain)
 
 
 def kernel_d(rows, hd, x, dy, bc, cols, cumt, stept, stepall, masks, mrow, sin, gin, cin, cw, skip, dtt, hp,
@@ -534,9 +575,13 @@
             cr = crow[:, r]
             gl = scan_lanes(arow[:, r], True) + scan_lanes(cr, False) - cr + grow[:, r]
             grad = (xrow[:, r] - rate * gl) * sigmoid(dtt[:, r] + hp[:, 0:1])
-            gdt[:, r] = grad
+            arow[:, r] = grad
             sums = sums + jnp.sum(grad, 1, keepdims=True)
             alog = alog - jnp.sum(gl * (rate * stepall[:, r]), 1, keepdims=True)
+        per = GW // hd
+        pieces = [arow[8 * g : 8 * g + per] for g in range(8)]
+        pieces.append(jnp.zeros((128 - 8 * per, rows), f32))
+        gdt[...] = jnp.concatenate(pieces, 0).T.astype(bf16)
         lane = lax.broadcasted_iota(jnp.int32, (64, 128), 1)
         hsum[...] = jnp.where(lane == 0, sums, jnp.where(lane == 1, alog, 0.0))
         gcw[TAPS + 1 : TAPS + 2] = jnp.zeros((1, GW), f32)
@@ -610,7 +655,7 @@
             pl.BlockSpec((HALO, GW), blk),
             pl.BlockSpec((8, GW), blk),
             pl.BlockSpec((8, GW), blk),
-            pl.BlockSpec((64, rows), full),
+            pl.BlockSpec((rows, 128), full),
             pl.BlockSpec((64, 128), full),
         ],
         out_shape=[
@@ -618,7 +663,7 @@
             jax.ShapeDtypeStruct((HALO, ch), f32),
             jax.ShapeDtypeStruct((8, ch), f32),
             jax.ShapeDtypeStruct((8, ch), f32),
-            jax.ShapeDtypeStruct((64, rows), f32),
+            jax.ShapeDtypeStruct((rows, 128), bf16),
             jax.ShapeDtypeStruct((64, 128), f32),
         ],
         scratch_shapes=[
@@ -644,6 +689,244 @@
     )(x, dy, bc, cols, cumt, stept, stept, masks, mrow, sin, gin, pc, cw, skip, dtt, hp)
 
 
+def call_grid(kernel, steps, in_specs, out_specs, out_shape, flops, size, args):
+    return pl.pallas_call(
+        kernel,
+        grid_spec=pltpu.PrefetchScalarGridSpec(num_scalar_prefetch=1, grid=(steps,), in_specs=in_specs, out_specs=out_specs),
+        out_shape=out_shape,
+        compiler_params=pltpu.CompilerParams(dimension_semantics=("arbitrary",)),
+        cost_estimate=pl.CostEstimate(flops=flops, bytes_accessed=size, transcendentals=0),
+    )(*args)
+
+
+def full2(i, me):
+    return (0, 0)
+
+
+def full3(i, me):
+    return (0, 0, 0)
+
+
+def block_xor(j, me, nq):
+    return jnp.where(j < nq, me[1], 1 - me[1]) * nq + jnp.bitwise_xor(lax.rem(j, nq), me[0])
+
+
+def pair_specs(shape, k):
+    nq, nw, _, dw, _ = shape
+    block = (1, nw, 1, dw, GW)
+    mine = pl.BlockSpec(block, lambda i, me: (jnp.minimum(i, nq - 1), 0, k, 0, 0))
+    other = pl.BlockSpec(block, lambda i, me: (jnp.maximum(i - nq, 0), 0, k, 0, 0))
+    return mine, other
+
+
+def by_core(me, body, mine, other):
+    @pl.when(me[1] == 0)
+    def _():
+        body(mine, other)
+
+    @pl.when(me[1] == 1)
+    def _():
+        body(other, mine)
+
+
+def kernel_gate(nq, me, nm, wx, wy, out):
+    i = pl.program_id(0)
+
+    @pl.when(i < nq)
+    def _():
+        out[...] = mm(nm[...], flat(wx[0, :, 0])).astype(bf16)
+
+    @pl.when(i >= nq)
+    def _():
+        out[...] = mm(nm[...], flat(wy[0, :, 0])).astype(bf16)
+
+
+def call_gate(me, nm, wx, wy, di):
+    rows = nm.shape[0]
+    nq = wx.shape[0]
+    specs = [pl.BlockSpec(nm.shape, full2), *pair_specs(wx.shape, 0)]
+    out = pl.BlockSpec((rows, GW), lambda i, me: (0, block_xor(i, me, nq)))
+    shape = jax.ShapeDtypeStruct((rows, di), bf16)
+    flops = 2 * rows * nm.shape[1] * di
+    return call_grid(functools.partial(kernel_gate, nq), 2 * nq, specs, out, shape, flops, 8000000, (me, nm, wx, wy))
+
+
+def kernel_gg(nq, me, cot, wx, wy, out):
+    dw = wx.shape[3]
+
+    def body(one, two):
+        for c, w in enumerate((one, two)):
+            total = None
+            for k in range(nq):
+                term = mm_nt(cot[jnp.bitwise_xor(me[0], k)], w[k, 0, 0])
+                total = term if total is None else total + term
+            out[:, c * dw : (c + 1) * dw] = total
+
+    by_core(me, body, wx, wy)
+
+
+def call_gg(me, cot4, wx, wy, di):
+    nq, nw, _, dw, _ = wx.shape
+    rows = cot4.shape[1]
+    block = pl.BlockSpec((nq, 1, 1, dw, GW), lambda i, me: (0, i, 1, 0, 0))
+    specs = [pl.BlockSpec(cot4.shape, full3), block, block]
+    out = pl.BlockSpec((rows, 2 * dw), lambda i, me: (0, i))
+    shape = jax.ShapeDtypeStruct((rows, di), f32)
+    flops = 2 * rows * nq * GW * di
+    return call_grid(functools.partial(kernel_gg, nq), nw, specs, out, shape, flops, 10000000, (me, cot4, wx, wy))
+
+
+def kernel_out(me, gated, wx, wy, x, out):
+    nw, dw = wx.shape[1], wx.shape[3]
+
+    def body(one, two):
+        total = x[...].astype(f32)
+        for k in range(nw):
+            for c, w in enumerate((one, two)):
+                at = (2 * k + c) * dw
+                total = total + mm(gated[:, at : at + dw], w[0, k, 0])
+        out[...] = total.astype(bf16)
+
+    by_core(me, body, wx, wy)
+
+
+def call_out(me, gated, wx, wy, x):
+    rows, d = x.shape
+    nq, nw, _, dw, _ = wx.shape
+    block = pl.BlockSpec((1, nw, 1, dw, GW), lambda i, me: (i, 0, 1, 0, 0))
+    cols = pl.BlockSpec((rows, GW), lambda i, me: (0, jnp.bitwise_xor(i, me[0])))
+    specs = [pl.BlockSpec(gated.shape, full2), block, block, cols]
+    shape = jax.ShapeDtypeStruct((rows, d), bf16)
+    return call_grid(kernel_out, nq, specs, cols, shape, 2 * rows * d * gated.shape[1], 8000000, (me, gated, wx, wy, x))
+
+
+def kernel_pair(me, nt, ggate, gated, cot, keep, send):
+    nq, _, _, dw, _ = keep.shape
+    first = mm(nt[...], ggate[...])
+    second = mm_tn(gated[...], cot[...])
+
+    def body(one, two):
+        for c, out in enumerate((one, two)):
+            for q in range(nq):
+                at = (c * nq + q) * GW
+                rel = jnp.bitwise_xor(me[0], q)
+                out[rel, 0, 0] = first[:, at : at + GW].astype(bf16)
+                out[rel, 0, 1] = second[c * dw : (c + 1) * dw, q * GW : (q + 1) * GW].astype(bf16)
+
+    by_core(me, body, keep, send)
+
+
+def call_pair(me, nt, ggate, gated, cot, shape):
+    nq, nw, _, dw, _ = shape
+    rows = cot.shape[0]
+    specs = [
+        pl.BlockSpec((dw, rows), lambda i, me: (i, 0)),
+        pl.BlockSpec(ggate.shape, full2),
+        pl.BlockSpec((rows, 2 * dw), lambda i, me: (0, i)),
+        pl.BlockSpec(cot.shape, full2),
+    ]
+    out = [pl.BlockSpec((nq, 1, 2, dw, GW), lambda i, me: (0, i, 0, 0, 0))] * 2
+    shapes = [jax.ShapeDtypeStruct(shape, bf16)] * 2
+    return call_grid(kernel_pair, nw, specs, out, shapes, 4300000000, 14000000, (me, nt, ggate, gated, cot))
+
+
+def kernel_late(me, nt, gci, gdt, keep, send):
+    nq = keep.shape[0]
+    dw = nt.shape[0]
+    di = gci.shape[1] - GW
+    e = dw // (2 * nq)
+    first = mm(nt[...], gci[...])
+    dt = mm(nt[...], gdt[...])
+
+    def body(one, two):
+        for c, out in enumerate((one, two)):
+            for q in range(nq):
+                b = c * nq + q
+                rel = jnp.bitwise_xor(me[0], q)
+                out[rel, 0, 0:dw] = first[:, b * GW : (b + 1) * GW].astype(bf16)
+                extra = [first[b * e : (b + 1) * e, di : di + GW]]
+                extra.append(jnp.concatenate([dt[b * e : b * e + e // 2], dt[b * e + e // 2 : (b + 1) * e]], 1))
+                short = out.shape[2] - dw - e - e // 2
+                if short:
+                    extra.append(jnp.zeros((short, GW), f32))
+                out[rel, 0, dw:] = jnp.concatenate(extra, 0).astype(bf16)
+
+    by_core(me, body, keep, send)
+
+
+def call_late(me, nt, gci, gdt, shape):
+    nq, nw, r, _ = shape
+    dw = nt.shape[0] // nw
+    specs = [
+        pl.BlockSpec((dw, nt.shape[1]), lambda i, me: (i, 0)),
+        pl.BlockSpec(gci.shape, full2),
+        pl.BlockSpec(gdt.shape, full2),
+    ]
+    out = [pl.BlockSpec((nq, 1, r, GW), lambda i, me: (0, i, 0, 0))] * 2
+    shapes = [jax.ShapeDtypeStruct(shape, bf16)] * 2
+    return call_grid(kernel_late, nw, specs, out, shapes, 2500000000, 8000000, (me, nt, gci, gdt))
+
+
+def kernel_gn_gate(nq, me, g, wx, wy, out):
+    i = pl.program_id(0)
+
+    @pl.when(i == 0)
+    def _():
+        out[...] = jnp.zeros_like(out)
+
+    @pl.when(i < nq)
+    def _():
+        out[...] += mm_nt(g[...], flat(wx[0, :, 0]))
+
+    @pl.when(i >= nq)
+    def _():
+        out[...] += mm_nt(g[...], flat(wy[0, :, 0]))
+
+
+def call_gn_gate(me, g, wx, wy):
+    rows = g.shape[0]
+    nq, nw, _, dw, _ = wx.shape
+    specs = [pl.BlockSpec((rows, GW), lambda i, me: (0, block_xor(i, me, nq))), *pair_specs(wx.shape, 0)]
+    out = pl.BlockSpec((rows, nw * dw), full2)
+    shape = jax.ShapeDtypeStruct((rows, nw * dw), f32)
+    return call_grid(functools.partial(kernel_gn_gate, nq), 2 * nq, specs, out, shape, 2200000000, 8000000, (me, g, wx, wy))
+
+
+def kernel_gn(nq, me, g, wx, wy, gbc, gdt, wb, start, out):
+    i = pl.program_id(0)
+
+    @pl.when(i == 0)
+    def _():
+        wide = flat(wb[...])
+        out[...] = start[...] + mm_nt(gbc[...], wide[:, 0:GW]) + mm_nt(gdt[...], wide[:, GW : GW + 128])
+
+    @pl.when(i < nq)
+    def _():
+        out[...] += mm_nt(g[...], flat(wx[0]))
+
+    @pl.when(i >= nq)
+    def _():
+        out[...] += mm_nt(g[...], flat(wy[0]))
+
+
+def call_gn(me, gci, wx, wy, gdt, wb, start):
+    rows = gci.shape[0]
+    nq = wx.shape[0]
+    block = (1,) + wx.shape[1:]
+    specs = [
+        pl.BlockSpec((rows, GW), lambda i, me: (0, block_of(i, me, nq))),
+        pl.BlockSpec(block, lambda i, me: (jnp.minimum(i, nq - 1), 0, 0, 0)),
+        pl.BlockSpec(block, lambda i, me: (jnp.maximum(i - nq, 0), 0, 0, 0)),
+        pl.BlockSpec((rows, GW), lambda i, me: (0, 2 * nq)),
+        pl.BlockSpec(gdt.shape, full2),
+        pl.BlockSpec(wb.shape, full3),
+        pl.BlockSpec(start.shape, full2),
+    ]
+    out = pl.BlockSpec(start.shape, full2)
+    shape = jax.ShapeDtypeStruct(start.shape, f32)
+    return call_grid(functools.partial(kernel_gn, nq), 2 * nq, specs, out, shape, 2500000000, 12000000, (me, gci, wx, wy, gci, gdt, wb, start))
+
+
 def slots(values, per):
     groups = values.shape[0] // per
     shaped = values.reshape((groups, per) + values.shape[1:])
@@ -656,29 +939,61 @@
     return values.reshape((groups, 8) + values.shape[1:])[:, :per].reshape((groups * per,) + values.shape[1:])
 
 
-def gather_small(value, axis):
-    count = lax.axis_size(axis)
-    wide = jnp.broadcast_to(value[None], (count,) + value.shape)
-    return lax.all_to_all(wide, axis, split_axis=0, concat_axis=0, tiled=True)
-
-
-def gather_weight(shard):
-    part = shard.shape[0] // lax.axis_size("seq")
-    mine = lax.dynamic_slice_in_dim(shard, lax.axis_index("seq") * part, part)
-    return lax.all_gather(mine, ("wsh", "seq"), axis=0, tiled=True)
-
-
-def reduce_weight(grad):
-    part = lax.psum_scatter(grad, "seq", scatter_dimension=0, tiled=True)
-    part = lax.psum_scatter(part, "wsh", scatter_dimension=0, tiled=True)
-    return lax.all_gather(part, "seq", axis=0, tiled=True)
-
-
-def local(x_in, seg_ids, in_weight, out_weight, conv_weight, conv_bias, dt_bias, a_log, skip_gain, norm_gain, gate_gain, cotangent):
-    nseq, nw = lax.axis_size("seq"), lax.axis_size("wsh")
-    me = lax.axis_index("seq")
+SEQ = ("q", "core")
+
+
+def swap(value, axis):
+    return lax.all_to_all(value, axis, split_axis=0, concat_axis=0, tiled=True)
+
+
+def gather(value, axis):
+    return swap(jnp.broadcast_to(value[None], (lax.axis_size(axis),) + value.shape), axis)
+
+
+def add_up(value, axis):
+    return jnp.sum(swap(value, axis).astype(f32), 0).astype(bf16)
+
+
+def partner(value, axis, k):
+    return lax.ppermute(value, axis, [(i, i ^ k) for i in range(lax.axis_size(axis))])
+
+
+def gather_xor(value, axis):
+    return jnp.stack([value] + [partner(value, axis, k) for k in range(1, lax.axis_size(axis))])
+
+
+def unxor(value, me):
+    n = value.shape[0]
+    bit = 1
+    while bit < n:
+        flipped = value.reshape((n // (2 * bit), 2, bit) + value.shape[1:])[:, ::-1].reshape(value.shape)
+        value = jnp.where((me & bit) != 0, flipped, value)
+        bit *= 2
+    return value
+
+
+def total_of(parts):
+    total = parts[0].astype(f32)
+    for part in parts[1:]:
+        total = total + part.astype(f32)
+    return total.astype(bf16)
+
+
+def reduce_plane(keep, send):
+    got = partner(send, "core", 1)
+    slots_q = [total_of((keep[k], got[k])) for k in range(keep.shape[0])]
+    parts = [slots_q[0]]
+    for k in range(1, keep.shape[0]):
+        parts.append(partner(slots_q[k], "q", k))
+    return total_of(parts)
+
+
+def layer(x_in, seg_ids, in_weight, out_weight, conv_weight, conv_bias, dt_bias, a_log, skip_gain, norm_gain, gate_gain, cotangent):
+    nq, nw = lax.axis_size("q"), lax.axis_size("wsh")
+    q_me, c_me = lax.axis_index("q"), lax.axis_index("core")
+    nseq = 2 * nq
     rows, d = x_in.shape[1:]
-    e = in_weight.shape[1]
+    dw = in_weight.shape[0]
     di = out_weight.shape[0] * nw
     heads = dt_bias.shape[0] * nw
     ch = conv_bias.shape[0] * nw
@@ -686,18 +1001,31 @@
     per = GW // hd
     ng = di // GW
     x, ids, cot = x_in[0], seg_ids[0], cotangent[0]
+    own = c_me * nq + q_me
 
     forward = [(i, i + 1) for i in range(nseq - 1)]
-    x_halo = lax.ppermute(x[rows - HALO :], "seq", forward)
-    id_halo = lax.ppermute(ids[rows - HALO :], "seq", forward)
-    id_halo = jnp.where(me == 0, -1, id_halo)
-
-    w_cd = gather_weight(in_weight[:, di:])
-    w_gate = gather_weight(in_weight[:, :di])
-    w_out = gather_weight(out_weight)
+    x_halo = lax.ppermute(x[rows - HALO :], SEQ, forward)
+    id_halo = lax.ppermute(ids[rows - HALO :], SEQ, forward)
+    id_halo = jnp.where(q_me + c_me == 0, -1, id_halo)
+
+    x_block = lax.dynamic_slice(in_weight, (0, di + own * GW), (dw, GW))
+    gate_block = lax.dynamic_slice(in_weight, (0, own * GW), (dw, GW))
+    out_block = lax.dynamic_slice(out_weight, (c_me * dw, q_me * GW), (dw, GW))
+    me = jnp.stack([q_me, c_me]).astype(jnp.int32)
+    wx0 = gather(gather(x_block, "wsh"), "q")
+    wx1 = partner(wx0, "core", 1)
     small = [conv_weight.reshape(-1), conv_bias, dt_bias, a_log, skip_gain, norm_gain, gate_gain]
     sizes = [s.shape[0] for s in small]
-    packed = gather_small(jnp.concatenate(small), "wsh")
+    lines = (sum(sizes) + 16 * 384 - 1) // (16 * 384) * 16
+    flat_small = jnp.pad(jnp.concatenate(small), (0, lines * 384 - sum(sizes))).reshape(lines, 384)
+    bcdt = jnp.pad(in_weight[:, 2 * di :], ((0, 0), (0, 384 - GW - heads)))
+    z_b = unxor(gather_xor(jnp.concatenate([bcdt, flat_small], 0), "wsh"), lax.axis_index("wsh"))
+    w_b = z_b[:, :dw]
+    packed = z_b[:, dw:].reshape(nw, lines * 384)
+    go_xor = gather_xor(jnp.stack([gate_block, out_block]), "wsh")
+    go_mine = unxor(go_xor, lax.axis_index("wsh"))
+    wg0 = gather_xor(go_mine, "q")
+    wg1 = partner(wg0, "core", 1)
     cut, at = [], 0
     for s in sizes:
         cut.append(packed[:, at : at + s].astype(f32))
@@ -724,51 +1052,58 @@
     xf = jnp.concatenate([x, x_halo], 0).astype(f32)
     rinv = lax.rsqrt(jnp.mean(xf * xf, 1, keepdims=True) + epsilon)
     normed = (xf * rinv * norm_g[None]).astype(bf16)
-    pc = mm(normed, w_cd).astype(bf16)
     normed_own = normed[:rows]
-    dtt = slots(pc[:rows, ch:].T.astype(f32), per)
-
-    xp, bc, s_loc, cumt, stept, cols = call_a(pc, cw, masks, mrow, dtt, hp, rows, di, hd)
-    recv = lax.all_to_all(s_loc, "seq", split_axis=0, concat_axis=0, tiled=True)
+    normed_t = normed_own.T
+
+    px, xp, bc, s_loc, cumt, stept, dtt, cols = call_a(me, normed, wx0, wx1, w_b, cw, masks, mrow, hp, rows, di, hd)
+    recv = swap(s_loc, SEQ)
     ya = call_b(xp, bc, cols, cumt, stept, masks, mrow, rows, hd, 0, ng // 2)
     s_all, dec = call_f(recv)
-    s_in = lax.all_to_all(s_all, "seq", split_axis=0, concat_axis=0, tiled=True)
+    s_in = swap(s_all, SEQ)
     yb = call_b(xp, bc, cols, cumt, stept, masks, mrow, rows, hd, ng // 2, ng - ng // 2)
 
-    gate = mm(normed_own, w_gate).astype(bf16)
-    gg = mm_nt(cot, w_out)
-    gated, gscan, ggate, ggain, g_loc = call_c(ya, yb, xp, bc, s_in, cols[7:9], gate, gg, skip, gain, rows, di, hd)
-    g_recv = lax.all_to_all(g_loc, "seq", split_axis=0, concat_axis=0, tiled=True)
+    gate = call_gate(me, normed_own, wg0, wg1, di)
+    gg = call_gg(me, cot.reshape(rows, nq, GW).transpose(1, 0, 2), wg0, wg1, di)
+    gated, gscan, ggate, ggain, g_loc = call_c(ya, yb, xp, bc, s_in, cols, gate, gg, skip, gain, rows, di, hd)
+    g_recv = swap(g_loc, SEQ)
+    output = call_out(me, gated, wg0, wg1, x)
     g_all = call_g(g_recv, dec)
-    g_in = lax.all_to_all(g_all, "seq", split_axis=0, concat_axis=0, tiled=True)
-
-    output = (x.astype(f32) + mm(gated, w_out)).astype(bf16)
-
-    def ordered(values):
-        r = values.shape[0] // (nw * nseq)
-        return values.reshape(nw, nseq, r, values.shape[1]).transpose(1, 0, 2, 3).reshape(values.shape)
-
-    r = d // (nw * nseq)
-    normed_t = normed_own.reshape(rows, nw, nseq, r).transpose(0, 2, 1, 3).reshape(rows, d)
-    grad_wout = reduce_weight(ordered(mm_tn(gated, cot).astype(bf16)))
-    grad_wgate = reduce_weight(mm_tn(normed_t, ggate).astype(bf16))
-    gn_gate = mm_nt(ggate, w_gate)
+    g_in = swap(g_all, SEQ)
+
+    early = call_pair(me, normed_t, ggate, gated, cot, (nq, nw, 2, dw, GW))
+    early = add_up(reduce_plane(*early), "wsh")
+    early = gather(early, SEQ)
+    gn_gate = call_gn_gate(me, ggate, wg0, wg1)
 
     gci, tail, rim, gcw, gdt, hsum = call_d(
-        xp, gscan, bc, cols, cumt, stept, masks, mrow, s_in, g_in, pc, cw, skip, dtt, hp, rows, di, hd
+        xp, gscan, bc, cols, cumt, stept, masks, mrow, s_in, g_in, px, cw, skip, dtt, hp, rows, di, hd
     )
-    backward = [(i + 1, i) for i in range(nseq - 1)]
-    rim_next = lax.ppermute(rim[8 - (TAPS - 1) :], "seq", backward)
+    rim_next = lax.ppermute(rim[8 - (TAPS - 1) :], SEQ, [(i + 1, i) for i in range(nseq - 1)])
     fixed = jnp.concatenate([tail[: HALO - (TAPS - 1)], tail[HALO - (TAPS - 1) :] + rim_next], 0)
     gci = lax.dynamic_update_slice(gci, fixed.astype(bf16), (rows - HALO, 0))
-    gcd = jnp.concatenate([gci, unslots(gdt, per).T.astype(bf16)], 1)
-    grad_wcd = reduce_weight(mm_tn(normed_t, gcd).astype(bf16))
-    gnorm = gn_gate + mm_nt(gcd, w_cd)
+    e = dw // nseq
+    r_late = dw + (e + e // 2 + 15) // 16 * 16
+    late = call_late(me, normed_t, gci, gdt, (nq, nw, r_late, GW))
+    late = add_up(reduce_plane(*late), "wsh")
+    late = gather(late, SEQ)
+    gnorm = call_gn(me, gci, wx0, wx1, gdt, w_b, gn_gate)
     x_own, rinv_own = xf[:rows], rinv[:rows]
     grad_norm = jnp.sum(gnorm * x_own * rinv_own, 0)
     gl = gnorm * norm_g[None]
     mean = jnp.mean(gl * x_own, 1, keepdims=True)
     grad_input = cot.astype(f32) + rinv_own * (gl - x_own * (rinv_own * rinv_own * mean))
+
+    def columns(blocks):
+        own_order = blocks.reshape(nq, 2, blocks.shape[1], GW).transpose(2, 1, 0, 3)
+        return own_order.reshape(blocks.shape[1], nseq * GW)
+
+    grad_gate = columns(early[:, 0])
+    grad_x = columns(late[:, :dw])
+    bcdt = late[:, dw:].reshape(nq, 2, r_late - dw, GW).transpose(1, 0, 2, 3)
+    grad_bc = bcdt[:, :, :e].reshape(dw, GW)
+    grad_dt = bcdt[:, :, e : e + e // 2].reshape(nseq, e // 2, 2, 128).transpose(0, 2, 1, 3).reshape(dw, 128)[:, :heads]
+    grad_win = jnp.concatenate([grad_gate, grad_x, grad_bc, grad_dt], 1).astype(f32)
+    grad_wout = early[:, 1].reshape(nq, 2, dw, GW).transpose(1, 2, 0, 3).reshape(2 * dw, d).astype(f32)
 
     pieces = [
         gcw[:TAPS].reshape(TAPS, nw, -1).transpose(1, 0, 2).reshape(nw, -1),
@@ -779,29 +1114,19 @@
         grad_norm.reshape(nw, -1),
         jnp.sum(ggain, 0).reshape(nw, -1),
     ]
-    stacked = lax.all_to_all(jnp.concatenate(pieces, 1), "wsh", split_axis=0, concat_axis=0, tiled=True)
-    total = jnp.sum(gather_small(jnp.sum(stacked, 0), "seq"), 0)
+    stacked = swap(jnp.concatenate(pieces, 1), "wsh")
+    total = jnp.sum(gather(jnp.sum(stacked, 0), SEQ), 0)
     outs, at = [], 0
     for s in sizes:
         outs.append(total[at : at + s])
         at += s
-    return (
-        output[None],
-        grad_input[None],
-        jnp.concatenate([grad_wgate, grad_wcd], 1).astype(f32),
-        grad_wout.astype(f32),
-        outs[0].reshape(TAPS, -1),
-        outs[1],
-        outs[2],
-        outs[3],
-        outs[4],
-        outs[5],
-        outs[6],
-    )
+    return (output[None], grad_input[None], grad_win, grad_wout, outs[0].reshape(TAPS, -1)) + tuple(outs[1:])
 
 
 def solution(mesh):
-    act, wide, vec = P("wsh", "seq", None), P("wsh", None), P("wsh")
-    in_specs = (act, P("wsh", "seq"), wide, wide, P(None, "wsh"), vec, vec, vec, vec, vec, vec, act)
+    nseq, nw = mesh.shape["seq"], mesh.shape["wsh"]
+    fine = jax.sharding.Mesh(mesh.devices.reshape(nseq // 2, 2, nw), ("q", "core", "wsh"))
+    act, wide, vec = P("wsh", SEQ, None), P("wsh", None), P("wsh")
+    in_specs = (act, P("wsh", SEQ), wide, wide, P(None, "wsh"), vec, vec, vec, vec, vec, vec, act)
     out_specs = (act, act, wide, wide, P(None, "wsh"), vec, vec, vec, vec, vec, vec)
-    return jax.shard_map(local, mesh=mesh, in_specs=in_specs, out_specs=out_specs, check_vma=False)
+    return jax.shard_map(layer, mesh=fine, in_specs=in_specs, out_specs=out_specs, check_vma=False)

time: 600 us -> 538 us (0.90)
  waiting for transfers between devices: 298 us -> 144 us
  Pallas kernels: 103 us -> 172 us
  matrix products: 55.6 us -> 0 us
  starting transfers between devices: 27.8 us -> 73.5 us
  other arithmetic: 20.5 us -> 48.7 us
  between operations: 15.2 us -> 1.68 us
  blocking collectives: 31.1 us -> 38.4 us
  local copies, waits for them, and re-layouts: 42.1 us -> 49 us
    all_gather x6 -> x0, waiting for transfers between devices: 170 us -> none  [the longest x3 138 us: gather_weight(): return lax.all_gather(mine, ('wsh', 'seq'), axis=0, tiled=True)]
    all_to_all x5 -> x9, waiting for transfers between devices: 7.73 us -> 108 us  [swap(): return lax.all_to_all(value, axis, split_axis=0, concat_axis=0, tiled=True)]
    pallas_call x1 -> x8, Pallas kernels: 13.5 us -> 82.6 us  [the longest x7 62.8 us: call_grid(): pl.pallas_call(kernel, grid_spec=pltpu.PrefetchScalarGridSpec(num_scalar_...]
    reduce_scatter x5 -> x0, waiting for transfers between devices: 61.3 us -> none  [the longest x3 61.2 us: reduce_weight(): part = lax.psum_scatter(part, 'wsh', scatter_dimension=0, tiled=True)]
    unnamed x13 -> x0, waiting for transfers between devices: 58.4 us -> none
    dot_general x9 -> x0, matrix products: 55.6 us -> none  [the longest x3 21.8 us: mm_nt(): lax.dot_general(a, b, (((1,), (1,)), ((), ())), preferred_element_type=f32)]
    ppermute x3 -> x22, waiting for transfers between devices: 0.01 us -> 36.6 us  [the longest x19 36.6 us: partner(): lax.ppermute(value, axis, [(i, i ^ k) for i in range(lax.axis_size(axis))])]
    ppermute x3 -> x22, starting transfers between devices: 7.08 us -> 34.6 us  [the longest x19 27.3 us: partner(): lax.ppermute(value, axis, [(i, i ^ k) for i in range(lax.axis_size(axis))])]
  transfers between devices with their start and end apart: 20 -> 31, of which waited for: 11 -> 9; matrix products, arithmetic and copies ran while one was open for 16% -> 15% of each run, Pallas kernels for 15% -> 20%
where the time goes in v2:
time: 538 us; the launch traced here: 528 us
  Pallas kernels  172 us (32%)
  waiting for transfers between devices  144 us (27%)
  starting transfers between devices  73.5 us (14%)
  local copies, waits for them, and re-layouts  49 us (9%)
  other arithmetic  48.7 us (9%)
  blocking collectives  38.4 us (7%)
    all_to_all x9, waiting for transfers between devices, swap(): return lax.all_to_all(value, axis, split_axis=0, concat_axis=0, tiled=True)  108 us
    pallas_call x7, Pallas kernels, call_grid(): pl.pallas_call(kernel, grid_spec=pltpu.PrefetchScalarGridSpec(num_scalar_...  62.8 us
    pallas_call x1, Pallas kernels, call_d(): pl.pallas_call(functools.partial(kernel_d, rows, hd), grid=(ng + 1,), in_...  50.6 us
    all_to_all x9, starting transfers between devices, swap(): return lax.all_to_all(value, axis, split_axis=0, concat_axis=0, tiled=True)  38.9 us
    all_to_all x3, blocking collectives, swap(): return lax.all_to_all(value, axis, split_axis=0, concat_axis=0, tiled=True)  38.4 us
    ppermute x19, waiting for transfers between devices, partner(): lax.ppermute(value, axis, [(i, i ^ k) for i in range(lax.axis_size(axis))])  36.6 us
    ppermute x19, starting transfers between devices, partner(): lax.ppermute(value, axis, [(i, i ^ k) for i in range(lax.axis_size(axis))])  27.3 us
    pallas_call x1, Pallas kernels, call_a(): pl.pallas_call(functools.partial(kernel_a, rows, hd, GW // hd, nq), grid_...  19.8 us
  transfers between devices with their start and end apart: 31, of which 9 were waited for; matrix products, arithmetic and copies ran while one was open for 15% of the time, Pallas kernels for 20%

profile of v2, /device:TPU:0, one launch (start us, length us, event | category | flops | bytes accessed | tf_op | source)
XLA Modules:
  0.0 527.6 jit_solution(474306846960221325)
XLA Ops:
  2.9 3.1 collective-permute-start.6
  6.0 2.6 collective-permute-start.7
  13.0 4.8 all-to-all-start
  24.4 4.5 collective-permute-start
  36.5 2.7 fusion.11
  44.3 8.5 %collective-permute-start.2 = (bf16[272,384]{1,0:T(8,128)(2,1)}, bf16[272,384]{1,0:T(8,128)(2,1)S(1)}, u32[]{:S(2)}, u32[]{:S(2)}) collective-permute-start(bf16[272,384]{1,0:T(8,128)(2,1)} %get-tuple-element.147), channel_id=1, source_target_pairs={{0,2},{1,3},{2,0},{3,1},{4,6},{5,7},{6,4},{7,5},{8,10},{9,11},{10,... | collective-permute-start | bytes 626696 | tf_op jit(solution)/shard_map/ppermute | solution.py:958
  54.7 8.0 %collective-permute-done.2 = bf16[272,384]{1,0:T(8,128)(2,1)S(1)} collective-permute-done((bf16[272,384]{1,0:T(8,128)(2,1)}, bf16[272,384]{1,0:T(8,128)(2,1)S(1)}, u32[]{:S(2)}, u32[]{:S(2)}) %collective-permute-start.2) | collective-permute-done | bytes 208928 | tf_op jit(solution)/shard_map/ppermute | solution.py:958
  65.6 2.6 broadcast_in_dim.72
  68.1 4.5 all-to-all-start.1
  74.0 24.9 %collective-permute-done.10 = bf16[4,2,256,256]{3,2,1,0:T(8,128)(2,1)} collective-permute-done((bf16[4,2,256,256]{3,2,1,0:T(8,128)(2,1)}, bf16[4,2,256,256]{3,2,1,0:T(8,128)(2,1)}, u32[]{:S(2)}, u32[]{:S(2)}) %collective-permute-start.10) | collective-permute-done | bytes 1048608 | tf_op jit(solution)/shard_map/ppermute | solution.py:958
  98.9 3.6 pad_maximum_fusion.wx
  105.2 5.0 all-to-all-done.1.wx
  116.2 19.8 %conv_state.1 = (bf16[528,2304]{1,0:T(8,128)(2,1)}, bf16[512,2048]{1,0:T(8,128)(2,1)}, bf16[512,256]{1,0:T(8,128)(2,1)}, bf16[8,144,256]{2,1,0:T(8,128)(2,1)}, f...) custom-call(s32[2]{0:T(128)} %pad_add_fusion.1.me, ...), custom_call_target="tpu_custom_call" | custom-call | flops 3000000000 | bytes 12000000 | tf_op jit(solution)/shard_map/conv_state/pallas_call | solution.py:190
  136.0 4.7 all-to-all-start.2
  143.4 9.7 %scan_forward.3.yb = f32[512,1024]{1,0:T(8,128)} custom-call(bf16[512,2048]{1,0:T(8,128)(2,1)} %get-tuple-element.36.x, bf16[512,256]{1,0:T(8,128)(2,1)} %get-tuple-element.37.bc, bf16[9,512,128]{2,1,0:T(8,128)(2,1)} %get-tuple-element.38.cols.whi.wlo, f32[64,512]{1,0:T(8,128)} %get-tuple-element.39.cumt, f32[64,512]{1,0:T(8,128)} %get-tuple-element.40.stept.stepall, ...), custom_call_target="tpu_custom_call" | custom-call | flops 800000000 | bytes 4000000 | tf_op jit(solution)/shard_map/scan_forward/pallas_call | solution.py:336
  155.1 4.2 all-to-all-start.3
  159.3 9.6 %scan_forward.2.ya = f32[512,1024]{1,0:T(8,128)} custom-call(bf16[512,2048]{1,0:T(8,128)(2,1)} %get-tuple-element.36.x, bf16[512,256]{1,0:T(8,128)(2,1)} %get-tuple-element.37.bc, bf16[9,512,128]{2,1,0:T(8,128)(2,1)} %get-tuple-element.38.cols.whi.wlo, f32[64,512]{1,0:T(8,128)} %get-tuple-element.39.cumt, f32[64,512]{1,0:T(8,128)} %get-tuple-element.40.stept.stepall, ...), custom_call_target="tpu_custom_call" | custom-call | flops 800000000 | bytes 4000000 | tf_op jit(solution)/shard_map/scan_forward/pallas_call | solution.py:336
  168.9 7.3 %shard_map.204.gg = f32[512,2048]{1,0:T(8,128)} custom-call(s32[2]{0:T(128)} %pad_add_fusion.1.me, bf16[4,512,256]{2,1,0:T(8,128)(2,1)} %bitcast.161, bf16[4,4,2,256,256]{4,3,2,1,0:T(8,128)(2,1)} %pad_maximum_fusion.wx, bf16[4,4,2,256,256]{4,3,2,1,0:T(8,128)(2,1)} %collective-permute-done.12.wy), custom_call_target="tpu_custom_call" | custom-call | flops 2147483648 | bytes 10000000 | tf_op jit(solution)/shard_map/pallas_call | solution.py:693
  176.2 9.0 %shard_map.203.gate = bf16[512,2048]{1,0:T(8,128)(2,1)} custom-call(s32[2]{0:T(128)} %pad_add_fusion.1.me, bf16[512,1024]{1,0:T(8,128)(2,1)} %copy.175.nm, bf16[4,4,2,256,256]{4,3,2,1,0:T(8,128)(2,1)} %pad_maximum_fusion.wx, bf16[4,4,2,256,256]{4,3,2,1,0:T(8,128)(2,1)} %collective-permute-done.12.wy), custom_call_target="tpu_custom_call" | custom-call | flops 2147483648 | bytes 8000000 | tf_op jit(solution)/shard_map/pallas_call | solution.py:693
  186.4 15.6 %gate_both.1 = (bf16[512,2048]{1,0:T(8,128)(2,1)}, bf16[512,2048]{1,0:T(8,128)(2,1)}, bf16[512,2048]{1,0:T(8,128)(2,1)}, f32[8,2048]{1,0:T(8,128)}, bf16[8,128,256]{2,1,0:T(8,128)(2,1)}) custom-call(f32[512,1024]{1,0:T(8,128)} %scan_forward.2.ya, f32[512,1024]{1,0:T(8,128)} %scan_forward.3.yb, bf16[512,2048]{1,0:T(8,128)(2,1)} %get-tuple-element.36.x, ...), custom_call_target="tpu_custom_call" | custom-call | flops 1200000000 | bytes 20000000 | tf_op jit(solution)/shard_map/gate_both/pallas_call | solution.py:424
  202.0 13.9 %all_to_all.65.recv = bf16[8,128,256]{2,1,0:T(8,128)(2,1)} all-to-all(bf16[8,128,256]{2,1,0:T(8,128)(2,1)} %get-tuple-element.45), channel_id=1, replica_groups=mesh['q'=4,'core'=2,'wsh'=4] {'q','core'}, dimensions={0} | all-to-all | bytes 1048576 | tf_op jit(solution)/shard_map/all_to_all | solution.py:946
  217.9 13.8 %all_to_all.66.gin = bf16[8,128,256]{2,1,0:T(8,128)(2,1)} all-to-all(bf16[8,128,256]{2,1,0:T(8,128)(2,1)} %join_backward.1), channel_id=1, replica_groups=mesh['q'=4,'core'=2,'wsh'=4] {'q','core'}, dimensions={0} | all-to-all | bytes 1048576 | tf_op jit(solution)/shard_map/all_to_all | solution.py:946
  231.8 50.6 %scan_backward.1 = (bf16[512,2304]{1,0:T(8,128)(2,1)}, f32[16,2304]{1,0:T(8,128)}, f32[8,2304]{1,0:T(8,128)}, f32[8,2304]{1,0:T(8,128)}, bf16[512,128]{1,0:T(8,128)(2,1)}, /*index=5*/f32[64,128]{1,0:T(8,128)}) custom-call(bf16[512,2048]{1,0:T(8,128)(2,1)} %get-tuple-element.36.x, bf16[512,2048]{1,0:T(8,128)(2,1)} %get-tuple-element.44.dy, ...), custom_call_target="tpu_custom_call" | custom-call | flops 4000000000 | bytes 14000000 | tf_op jit(solution)/shard_map/scan_backward/pallas_call | solution.py:632
  284.8 10.5 %shard_map.208 = (bf16[4,4,2,256,256]{4,3,2,1,0:T(8,128)(2,1)}, bf16[4,4,2,256,256]{4,3,2,1,0:T(8,128)(2,1)}) custom-call(s32[2]{0:T(128)} %pad_add_fusion.1.me, bf16[1024,512]{1,0:T(8,128)(2,1)} %get-tuple-element.141.nt, bf16[512,2048]{1,0:T(8,128)(2,1)} %get-tuple-element.53.g.ggate, bf16[512,2048]{1,0:T(8,128)(2,1)} %get-tuple-element.43.gated, ...), custom_call_target="tpu_custom_call" | custom-call | flops 4300000256 | bytes 14000000 | tf_op jit(solution)/shard_map/pallas_call | solution.py:693
  297.1 7.8 %shard_map.209 = (bf16[4,4,304,256]{3,2,1,0:T(8,128)(2,1)}, bf16[4,4,304,256]{3,2,1,0:T(8,128)(2,1)}) custom-call(s32[2]{0:T(128)} %pad_add_fusion.1.me, bf16[1024,512]{1,0:T(8,128)(2,1)} %get-tuple-element.141.nt, bf16[512,2304]{1,0:T(8,128)(2,1)} %maximum_dynamic-update-slice_fusion.g.gbc.gci, bf16[512,128]{1,0:T(8,128)(2,1)} %get-tuple-element.52.gdt), custom_call_target="tpu_custom_call" | custom-call | flops 2500000000 | bytes 8000000 | tf_op jit(solution)/shard_map/pallas_call | solution.py:693
  305.0 2.7 maximum_convert_fusion.1
  307.7 9.6 %shard_map.206.start = f32[512,1024]{1,0:T(8,128)} custom-call(s32[2]{0:T(128)} %pad_add_fusion.1.me, bf16[512,2048]{1,0:T(8,128)(2,1)} %get-tuple-element.53.g.ggate, bf16[4,4,2,256,256]{4,3,2,1,0:T(8,128)(2,1)} %pad_maximum_fusion.wx, bf16[4,4,2,256,256]{4,3,2,1,0:T(8,128)(2,1)} %collective-permute-done.12.wy), custom_call_target="tpu_custom_call" | custom-call | flops 2200000000 | bytes 8000000 | tf_op jit(solution)/shard_map/pallas_call | solution.py:693
  317.4 3.0 fusion.14
  322.4 11.3 %shard_map.207 = f32[512,1024]{1,0:T(8,128)} custom-call(s32[2]{0:T(128)} %pad_add_fusion.1.me, bf16[512,2304]{1,0:T(8,128)(2,1)} %maximum_dynamic-update-slice_fusion.g.gbc.gci, bf16[4,4,256,256]{3,2,1,0:T(8,128)(2,1)} %all-to-all-done.1.wx, bf16[4,4,256,256]{3,2,1,0:T(8,128)(2,1)} %collective-permute-done.4.wy, ...), custom_call_target="tpu_custom_call" | custom-call | flops 2500000000 | bytes 12000000 | tf_op jit(solution)/shard_map/pallas_call | solution.py:693
  338.3 5.2 fusion.7
  347.8 10.6 %all_to_all.67 = f32[4,1,3672]{2,1,0:T(1,128)S(1)} all-to-all(f32[4,1,3672]{2,1,0:T(1,128)S(1)} %copy.195), channel_id=1, replica_groups=mesh['q'=4,'core'=2,'wsh'=4] {'wsh'}, dimensions={0} | all-to-all | bytes 117504 | tf_op jit(solution)/shard_map/all_to_all | solution.py:946
  359.2 3.4 all-to-all-start.11
  362.6 3.6 collective-permute-done.20
  366.2 2.9 fusion.5
  369.1 42.1 %all-to-all-done.11 = f32[8,1,3672]{2,1,0:T(1,128)S(1)} async-done(((f32[8,1,3672]{2,1,0:T(1,128)}), f32[8,1,3672]{2,1,0:T(1,128)S(1)}, u32[]{:S(2)}, u32[]{:S(2)}) %all-to-all-start.11) | async-done | bytes 117536 | tf_op jit(solution)/shard_map/all_to_all | solution.py:946
  411.2 5.1 all-to-all-start.8
  416.4 4.2 fusion.2
  420.5 12.5 %all-to-all-done.8 = bf16[4,304,256]{2,1,0:T(8,128)(2,1)S(1)} async-done(((bf16[4,304,256]{2,1,0:T(8,128)(2,1)}), bf16[4,304,256]{2,1,0:T(8,128)(2,1)S(1)}, u32[]{:S(2)}, u32[]{:S(2)}) %all-to-all-start.8) | async-done | bytes 622624 | tf_op jit(solution)/shard_map/all_to_all | solution.py:946
  433.8 3.5 all-to-all-start.6
  438.5 24.1 %all-to-all-done.6 = bf16[4,2,256,256]{3,2,1,0:T(8,128)(2,1)S(1)} async-done(((bf16[4,2,256,256]{3,2,1,0:T(8,128)(2,1)}), bf16[4,2,256,256]{3,2,1,0:T(8,128)(2,1)S(1)}, u32[]{:S(2)}, u32[]{:S(2)}) %all-to-all-start.6) | async-done | bytes 1048608 | tf_op jit(solution)/shard_map/all_to_all | solution.py:946
  463.7 4.3 all-to-all-start.9
  468.3 17.2 %all-to-all-done.9 = bf16[8,304,256]{2,1,0:T(8,128)(2,1)} async-done(((bf16[8,304,256]{2,1,0:T(8,128)(2,1)}), bf16[8,304,256]{2,1,0:T(8,128)(2,1)}, u32[]{:S(2)}, u32[]{:S(2)}) %all-to-all-start.9) | async-done | bytes 1245216 | tf_op jit(solution)/shard_map/all_to_all | solution.py:946
  487.1 4.6 all-to-all-start.7
  491.7 7.3 %shard_map.205 = bf16[512,1024]{1,0:T(8,128)(2,1)} custom-call(s32[2]{0:T(128)} %pad_add_fusion.1.me, bf16[512,2048]{1,0:T(8,128)(2,1)} %get-tuple-element.43.gated, bf16[4,4,2,256,256]{4,3,2,1,0:T(8,128)(2,1)} %pad_maximum_fusion.wx, bf16[4,4,2,256,256]{4,3,2,1,0:T(8,128)(2,1)} %collective-permute-done.12.wy, bf16[512,1024]{1,0:T(8,128)(2,1)} %bitcast.155), custom_call_target="tpu_custom_call" | custom-call | flops 2147483648 | bytes 8000000 | tf_op jit(solution)/shard_map/pallas_call | solution.py:693
  499.0 3.4 add_bitcast_fusion
  502.4 2.9 copy.197
  511.5 6.8 %all-to-all-done.7 = bf16[8,2,256,256]{3,2,1,0:T(8,128)(2,1)} async-done(((bf16[8,2,256,256]{3,2,1,0:T(8,128)(2,1)}), bf16[8,2,256,256]{3,2,1,0:T(8,128)(2,1)}, u32[]{:S(2)}, u32[]{:S(2)}) %all-to-all-start.7) | async-done | bytes 2097184 | tf_op jit(solution)/shard_map/all_to_all | solution.py:946
  518.3 2.7 fusion.25
  (242 shorter events, 81.9 us)
Async XLA Ops:
  0.7 7.9 %slice-start = ((bf16[256,4384]{0,1:T(8,128)(2,1)}), bf16[256,288]{0,1:T(8,128)(2,1)S(1)}, s32[]{:S(2)}) async-start(bf16[256,4384]{0,1:T(8,128)(2,1)} %param.14), calls=%async_computation.12 | async-start | bytes 294912 | tf_op jit(solution)/shard_map/slice | solution.py:1021
  0.7 8.1 %copy-start.22 = (bf16[4,576]{1,0:T(4,128)(2,1)S(1)}, bf16[4,576]{1,0:T(4,128)(2,1)}, u32[]{:S(2)}) copy-start(bf16[4,576]{1,0:T(4,128)(2,1)} %param.16) | copy-start | bytes 13828
  0.7 8.2 %copy-start.23 = (bf16[576]{0:T(1024)(128)(2,1)S(1)}, bf16[576]{0:T(1024)(128)(2,1)}, u32[]{:S(2)}) copy-start(bf16[576]{0:T(1024)(128)(2,1)} %param.17) | copy-start | bytes 3460
  0.7 8.2 %copy-start.25 = (bf16[8]{0:T(256)(128)(2,1)S(1)}, bf16[8]{0:T(256)(128)(2,1)}, u32[]{:S(2)}) copy-start(bf16[8]{0:T(256)(128)(2,1)} %param.18) | copy-start | bytes 52
  0.7 8.2 %copy-start.26 = (bf16[8]{0:T(256)(128)(2,1)S(1)}, bf16[8]{0:T(256)(128)(2,1)}, u32[]{:S(2)}) copy-start(bf16[8]{0:T(256)(128)(2,1)} %param.19) | copy-start | bytes 52
  0.7 8.2 %copy-start.27 = (bf16[8]{0:T(256)(128)(2,1)S(1)}, bf16[8]{0:T(256)(128)(2,1)}, u32[]{:S(2)}) copy-start(bf16[8]{0:T(256)(128)(2,1)} %param.20) | copy-start | bytes 52
  0.7 8.2 %copy-start.28 = (bf16[256]{0:T(256)(128)(2,1)S(1)}, bf16[256]{0:T(256)(128)(2,1)}, u32[]{:S(2)}) copy-start(bf16[256]{0:T(256)(128)(2,1)} %param.21) | copy-start | bytes 1540
  0.7 8.2 %copy-start.24 = (bf16[512]{0:T(512)(128)(2,1)S(1)}, bf16[512]{0:T(512)(128)(2,1)}, u32[]{:S(2)}) copy-start(bf16[512]{0:T(512)(128)(2,1)} %param.22) | copy-start | bytes 3076
  0.7 10.0 %copy-start.21 = (s32[1,512]{1,0:T(1,128)S(1)}, s32[1,512]{1,0:T(1,128)}, u32[]{:S(2)}) copy-start(s32[1,512]{1,0:T(1,128)} %param.13) | copy-start | bytes 6148
  2.9 28.8 %collective-permute-start.6 = (bf16[2,256,256]{2,1,0:T(8,128)(2,1)}, bf16[2,256,256]{2,1,0:T(8,128)(2,1)S(1)}, u32[]{:S(2)}, u32[]{:S(2)}) collective-permute-start(bf16[2,256,256]{2,1,0:T(8,128)(2,1)} %get-tuple-element.145), channel_id=1, source_target_pairs={{0,1},{1,0},{2,3},{3,2},{4,5},{5,4},{6,7},{7,6},{8,9},{9,8},{10,11... | collective-permute-start | bytes 786440 | tf_op jit(solution)/shard_map/ppermute | solution.py:958
  6.0 25.8 %collective-permute-start.7 = (bf16[2,256,256]{2,1,0:T(8,128)(2,1)}, bf16[2,256,256]{2,1,0:T(8,128)(2,1)S(1)}, u32[]{:S(2)}, u32[]{:S(2)}) collective-permute-start(bf16[2,256,256]{2,1,0:T(8,128)(2,1)} %get-tuple-element.145), channel_id=1, source_target_pairs={{0,2},{1,3},{2,0},{3,1},{4,6},{5,7},{6,4},{7,5},{8,10},{9,11},{10,... | collective-permute-start | bytes 786440 | tf_op jit(solution)/shard_map/ppermute | solution.py:958
  8.6 23.2 %collective-permute-start.8 = (bf16[2,256,256]{2,1,0:T(8,128)(2,1)}, bf16[2,256,256]{2,1,0:T(8,128)(2,1)S(1)}, u32[]{:S(2)}, u32[]{:S(2)}) collective-permute-start(bf16[2,256,256]{2,1,0:T(8,128)(2,1)} %get-tuple-element.145), channel_id=1, source_target_pairs={{0,3},{1,2},{2,1},{3,0},{4,7},{5,6},{6,5},{7,4},{8,11},{9,10},{10,... | collective-permute-start | bytes 786440 | tf_op jit(solution)/shard_map/ppermute | solution.py:958
  9.8 44.2 %collective-permute-start.1 = (bf16[272,384]{1,0:T(8,128)(2,1)}, bf16[272,384]{1,0:T(8,128)(2,1)}, u32[]{:S(2)}, u32[]{:S(2)}) collective-permute-start(bf16[272,384]{1,0:T(8,128)(2,1)} %get-tuple-element.147), channel_id=1, source_target_pairs={{0,1},{1,0},{2,3},{3,2},{4,5},{5,4},{6,7},{7,6},{8,9},{9,8},{10,11... | collective-permute-start | bytes 626696 | tf_op jit(solution)/shard_map/ppermute | solution.py:958
  10.8 13.6 %collective-permute-start.5 = (s32[16]{0:T(128)S(1)}, s32[16]{0:T(128)S(1)}, u32[]{:S(2)}, u32[]{:S(2)}) collective-permute-start(s32[16]{0:T(128)S(1)} %slice_bitcast_fusion.2), channel_id=1, source_target_pairs={{0,4},{4,8},{8,12},{12,16},{16,20},{20,24},{24,28},{1,5},{5,9},{9,... | collective-permute-start | bytes 200 | tf_op jit(solution)/shard_map/ppermute | solution.py:1008
  13.0 52.5 %all-to-all-start = ((bf16[4,256,256]{2,1,0:T(8,128)(2,1)}), bf16[4,256,256]{2,1,0:T(8,128)(2,1)}, u32[]{:S(2)}, u32[]{:S(2)}) async-start(bf16[4,256,256]{2,1,0:T(8,128)(2,1)} %broadcast_in_dim.71), calls=%async_computation | async-start | bytes 1048576 | tf_op jit(solution)/shard_map/all_to_all | solution.py:946
  18.4 3.9 copy-start.6
  24.4 19.9 %collective-permute-start = (bf16[16,1024]{0,1:T(8,128)(2,1)}, bf16[16,1024]{0,1:T(8,128)(2,1)}, u32[]{:S(2)}, u32[]{:S(2)}) collective-permute-start(bf16[16,1024]{0,1:T(8,128)(2,1)} %slice_bitcast_fusion), channel_id=1, source_target_pairs={{0,4},{4,8},{8,12},{12,16},{16,20},{20,24},{24,28},{1,5},{5,9},{9,... | collective-permute-start | bytes 98312 | tf_op jit(solution)/shard_map/ppermute | solution.py:1007
  39.1 34.8 %collective-permute-start.9 = (bf16[4,2,256,256]{3,2,1,0:T(8,128)(2,1)}, bf16[4,2,256,256]{3,2,1,0:T(8,128)(2,1)}, u32[]{:S(2)}, u32[]{:S(2)}) collective-permute-start(bf16[4,2,256,256]{3,2,1,0:T(8,128)(2,1)} %fusion.11), channel_id=1, source_target_pairs={{0,8},{8,0},{16,24},{24,16},{1,9},{9,1},{17,25},{25,17},{2,10},{10... | collective-permute-start | bytes 3145736 | tf_op jit(solution)/shard_map/ppermute | solution.py:958
  39.9 58.9 %collective-permute-start.10 = (bf16[4,2,256,256]{3,2,1,0:T(8,128)(2,1)}, bf16[4,2,256,256]{3,2,1,0:T(8,128)(2,1)}, u32[]{:S(2)}, u32[]{:S(2)}) collective-permute-start(bf16[4,2,256,256]{3,2,1,0:T(8,128)(2,1)} %fusion.11), channel_id=1, source_target_pairs={{0,16},{8,24},{16,0},{24,8},{1,17},{9,25},{17,1},{25,9},{2,18},{10... | collective-permute-start | bytes 3145736 | tf_op jit(solution)/shard_map/ppermute | solution.py:958
  40.1 58.7 %collective-permute-start.11 = (bf16[4,2,256,256]{3,2,1,0:T(8,128)(2,1)}, bf16[4,2,256,256]{3,2,1,0:T(8,128)(2,1)}, u32[]{:S(2)}, u32[]{:S(2)}) collective-permute-start(bf16[4,2,256,256]{3,2,1,0:T(8,128)(2,1)} %fusion.11), channel_id=1, source_target_pairs={{0,24},{8,16},{16,8},{24,0},{1,25},{9,17},{17,9},{25,1},{2,26},{10... | collective-permute-start | bytes 3145736 | tf_op jit(solution)/shard_map/ppermute | solution.py:958
  44.3 18.4 %collective-permute-start.2 = (bf16[272,384]{1,0:T(8,128)(2,1)}, bf16[272,384]{1,0:T(8,128)(2,1)S(1)}, u32[]{:S(2)}, u32[]{:S(2)}) collective-permute-start(bf16[272,384]{1,0:T(8,128)(2,1)} %get-tuple-element.147), channel_id=1, source_target_pairs={{0,2},{1,3},{2,0},{3,1},{4,6},{5,7},{6,4},{7,5},{8,10},{9,11},{10,... | collective-permute-start | bytes 626696 | tf_op jit(solution)/shard_map/ppermute | solution.py:958
  54.1 8.6 %collective-permute-start.3 = (bf16[272,384]{1,0:T(8,128)(2,1)}, bf16[272,384]{1,0:T(8,128)(2,1)S(1)}, u32[]{:S(2)}, u32[]{:S(2)}) collective-permute-start(bf16[272,384]{1,0:T(8,128)(2,1)} %get-tuple-element.147), channel_id=1, source_target_pairs={{0,3},{1,2},{2,1},{3,0},{4,7},{5,6},{6,5},{7,4},{8,11},{9,10},{10,... | collective-permute-start | bytes 626696 | tf_op jit(solution)/shard_map/ppermute | solution.py:958
  62.7 5.4 %copy-start.14 = (bf16[272,384]{1,0:T(8,128)(2,1)}, bf16[272,384]{1,0:T(8,128)(2,1)S(1)}, u32[]{:S(2)}) copy-start(bf16[272,384]{1,0:T(8,128)(2,1)S(1)} %collective-permute-done.2) | copy-start | bytes 626692
  68.1 42.1 %all-to-all-start.1 = ((bf16[4,4,256,256]{3,2,1,0:T(8,128)(2,1)}), bf16[4,4,256,256]{3,2,1,0:T(8,128)(2,1)}, u32[]{:S(2)}, u32[]{:S(2)}) async-start(bf16[4,4,256,256]{3,2,1,0:T(8,128)(2,1)} %broadcast_in_dim.72), calls=%async_computation.1 | async-start | bytes 4194304 | tf_op jit(solution)/shard_map/all_to_all | solution.py:946
  102.5 66.4 %collective-permute-start.12 = (bf16[4,4,2,256,256]{4,3,2,1,0:T(8,128)(2,1)}, bf16[4,4,2,256,256]{4,3,2,1,0:T(8,128)(2,1)}, u32[]{:S(2)}, u32[]{:S(2)}) collective-permute-start(bf16[4,4,2,256,256]{4,3,2,1,0:T(8,128)(2,1)} %pad_maximum_fusion.wx), channel_id=1, source_target_pairs={{0,4},{4,0},{1,5},{5,1},{2,6},{6,2},{3,7},{7,3},{8,12},{12,8},{9,1... | collective-permute-start | bytes 12582920 | tf_op jit(solution)/shard_map/ppermute | solution.py:958
  110.3 5.9 %collective-permute-start.4 = (bf16[4,4,256,256]{3,2,1,0:T(8,128)(2,1)}, bf16[4,4,256,256]{3,2,1,0:T(8,128)(2,1)}, u32[]{:S(2)}, u32[]{:S(2)}) collective-permute-start(bf16[4,4,256,256]{3,2,1,0:T(8,128)(2,1)} %all-to-all-done.1.wx), channel_id=1, source_target_pairs={{0,4},{4,0},{1,5},{5,1},{2,6},{6,2},{3,7},{7,3},{8,12},{12,8},{9,1... | collective-permute-start | bytes 6291464 | tf_op jit(solution)/shard_map/ppermute | solution.py:958
  136.0 17.1 %all-to-all-start.2 = ((bf16[8,144,256]{2,1,0:T(8,128)(2,1)}), bf16[8,144,256]{2,1,0:T(8,128)(2,1)}, u32[]{:S(2)}, u32[]{:S(2)}) async-start(bf16[8,144,256]{2,1,0:T(8,128)(2,1)} %get-tuple-element.41), calls=%async_computation.2 | async-start | bytes 1179648 | tf_op jit(solution)/shard_map/all_to_all | solution.py:946
  155.1 30.0 %all-to-all-start.3 = ((bf16[8,128,256]{2,1,0:T(8,128)(2,1)}), bf16[8,128,256]{2,1,0:T(8,128)(2,1)S(1)}, u32[]{:S(2)}, u32[]{:S(2)}) async-start(bf16[8,128,256]{2,1,0:T(8,128)(2,1)} %get-tuple-element.42), calls=%async_computation.3 | async-start | bytes 1048576 | tf_op jit(solution)/shard_map/all_to_all | solution.py:946
  283.3 13.1 %collective-permute-start.13 = (f32[3,2304]{1,0:T(4,128)S(1)}, f32[3,2304]{1,0:T(4,128)S(1)}, u32[]{:S(2)}, u32[]{:S(2)}) collective-permute-start(f32[3,2304]{1,0:T(4,128)S(1)} %slice.225), channel_id=1, source_target_pairs={{4,0},{8,4},{12,8},{16,12},{20,16},{24,20},{28,24},{5,1},{9,5},{13... | collective-permute-start | bytes 82952 | tf_op jit(solution)/shard_map/ppermute | solution.py:1081
  284.8 11.6 %copy-start.18 = (f32[16,2304]{1,0:T(8,128)S(1)}, f32[16,2304]{1,0:T(8,128)}, u32[]{:S(2)}) copy-start(f32[16,2304]{1,0:T(8,128)} %get-tuple-element.50) | copy-start | bytes 442372
  295.3 43.0 %collective-permute-start.14 = (bf16[4,4,2,256,256]{4,3,2,1,0:T(8,128)(2,1)}, bf16[4,4,2,256,256]{4,3,2,1,0:T(8,128)(2,1)}, u32[]{:S(2)}, u32[]{:S(2)}) collective-permute-start(bf16[4,4,2,256,256]{4,3,2,1,0:T(8,128)(2,1)} %get-tuple-element.55), channel_id=1, source_target_pairs={{0,4},{4,0},{1,5},{5,1},{2,6},{6,2},{3,7},{7,3},{8,12},{12,8},{9,1... | collective-permute-start | bytes 12582920 | tf_op jit(solution)/shard_map/ppermute | solution.py:958
  304.9 12.4 %collective-permute-start.18 = (bf16[4,4,304,256]{3,2,1,0:T(8,128)(2,1)}, bf16[4,4,304,256]{3,2,1,0:T(8,128)(2,1)}, u32[]{:S(2)}, u32[]{:S(2)}) collective-permute-start(bf16[4,4,304,256]{3,2,1,0:T(8,128)(2,1)} %get-tuple-element.57), channel_id=1, source_target_pairs={{0,4},{4,0},{1,5},{5,1},{2,6},{6,2},{3,7},{7,3},{8,12},{12,8},{9,1... | collective-permute-start | bytes 7471112 | tf_op jit(solution)/shard_map/ppermute | solution.py:958
  307.7 9.7 %copy-start.20 = (f32[8,2304]{1,0:T(8,128)S(1)}, f32[8,2304]{1,0:T(8,128)}, u32[]{:S(2)}) copy-start(f32[8,2304]{1,0:T(8,128)} %get-tuple-element.58) | copy-start | bytes 221188
  307.7 9.7 %copy-start.9 = (bf16[4,4,304,256]{3,2,1,0:T(8,128)(2,1)S(1)}, bf16[4,4,304,256]{3,2,1,0:T(8,128)(2,1)}, u32[]{:S(2)}) copy-start(bf16[4,4,304,256]{3,2,1,0:T(8,128)(2,1)} %get-tuple-element.56) | copy-start | bytes 7471108
  317.4 3.9 copy-start.17
  320.4 24.5 %collective-permute-start.19 = (bf16[4,304,256]{2,1,0:T(8,128)(2,1)}, bf16[4,304,256]{2,1,0:T(8,128)(2,1)S(1)}, u32[]{:S(2)}, u32[]{:S(2)}) collective-permute-start(bf16[4,304,256]{2,1,0:T(8,128)(2,1)} %get-tuple-element.134), channel_id=1, source_target_pairs={{0,8},{8,0},{16,24},{24,16},{1,9},{9,1},{17,25},{25,17},{2,10},{10... | collective-permute-start | bytes 1867784 | tf_op jit(solution)/shard_map/ppermute | solution.py:958
  335.6 30.6 %collective-permute-start.20 = (bf16[4,304,256]{2,1,0:T(8,128)(2,1)}, bf16[4,304,256]{2,1,0:T(8,128)(2,1)}, u32[]{:S(2)}, u32[]{:S(2)}) collective-permute-start(bf16[4,304,256]{2,1,0:T(8,128)(2,1)} %get-tuple-element.136), channel_id=1, source_target_pairs={{0,16},{8,24},{16,0},{24,8},{1,17},{9,25},{17,1},{25,9},{2,18},{10... | collective-permute-start | bytes 1867784 | tf_op jit(solution)/shard_map/ppermute | solution.py:958
  336.3 30.0 %collective-permute-start.21 = (bf16[4,304,256]{2,1,0:T(8,128)(2,1)}, bf16[4,304,256]{2,1,0:T(8,128)(2,1)}, u32[]{:S(2)}, u32[]{:S(2)}) collective-permute-start(bf16[4,304,256]{2,1,0:T(8,128)(2,1)} %get-tuple-element.135), channel_id=1, source_target_pairs={{0,24},{8,16},{16,8},{24,0},{1,25},{9,17},{17,9},{25,1},{2,26},{10... | collective-permute-start | bytes 1867784 | tf_op jit(solution)/shard_map/ppermute | solution.py:958
  338.3 8.7 %copy-start.2 = (f32[528,1024]{0,1:T(8,128)S(1)}, f32[528,1024]{0,1:T(8,128)}, u32[]{:S(2)}) copy-start(f32[528,1024]{0,1:T(8,128)} %maximum_convert_fusion.1) | copy-start | bytes 6488068
  343.5 72.9 %collective-permute-start.15 = (bf16[4,2,256,256]{3,2,1,0:T(8,128)(2,1)}, bf16[4,2,256,256]{3,2,1,0:T(8,128)(2,1)}, u32[]{:S(2)}, u32[]{:S(2)}) collective-permute-start(bf16[4,2,256,256]{3,2,1,0:T(8,128)(2,1)} %get-tuple-element.131), channel_id=1, source_target_pairs={{0,8},{8,0},{16,24},{24,16},{1,9},{9,1},{17,25},{25,17},{2,10},{10... | collective-permute-start | bytes 3145736 | tf_op jit(solution)/shard_map/ppermute | solution.py:958
  344.3 72.0 %collective-permute-start.16 = (bf16[4,2,256,256]{3,2,1,0:T(8,128)(2,1)}, bf16[4,2,256,256]{3,2,1,0:T(8,128)(2,1)}, u32[]{:S(2)}, u32[]{:S(2)}) collective-permute-start(bf16[4,2,256,256]{3,2,1,0:T(8,128)(2,1)} %get-tuple-element.133), channel_id=1, source_target_pairs={{0,16},{8,24},{16,0},{24,8},{1,17},{9,25},{17,1},{25,9},{2,18},{10... | collective-permute-start | bytes 3145736 | tf_op jit(solution)/shard_map/ppermute | solution.py:958
  344.9 71.4 %collective-permute-start.17 = (bf16[4,2,256,256]{3,2,1,0:T(8,128)(2,1)}, bf16[4,2,256,256]{3,2,1,0:T(8,128)(2,1)}, u32[]{:S(2)}, u32[]{:S(2)}) collective-permute-start(bf16[4,2,256,256]{3,2,1,0:T(8,128)(2,1)} %get-tuple-element.132), channel_id=1, source_target_pairs={{0,24},{8,16},{16,8},{24,0},{1,25},{9,17},{17,9},{25,1},{2,26},{10... | collective-permute-start | bytes 3145736 | tf_op jit(solution)/shard_map/ppermute | solution.py:958
  359.2 52.0 %all-to-all-start.11 = ((f32[8,1,3672]{2,1,0:T(1,128)}), f32[8,1,3672]{2,1,0:T(1,128)S(1)}, u32[]{:S(2)}, u32[]{:S(2)}) async-start(f32[8,1,3672]{2,1,0:T(1,128)} %broadcast_in_dim.87), calls=%async_computation.11 | async-start | bytes 237568 | tf_op jit(solution)/shard_map/all_to_all | solution.py:946
  411.2 21.8 %all-to-all-start.8 = ((bf16[4,304,256]{2,1,0:T(8,128)(2,1)}), bf16[4,304,256]{2,1,0:T(8,128)(2,1)S(1)}, u32[]{:S(2)}, u32[]{:S(2)}) async-start(bf16[4,304,256]{2,1,0:T(8,128)(2,1)} %fusion.5), calls=%async_computation.8 | async-start | bytes 1245184 | tf_op jit(solution)/shard_map/all_to_all | solution.py:946
  433.8 28.8 %all-to-all-start.6 = ((bf16[4,2,256,256]{3,2,1,0:T(8,128)(2,1)}), bf16[4,2,256,256]{3,2,1,0:T(8,128)(2,1)S(1)}, u32[]{:S(2)}, u32[]{:S(2)}) async-start(bf16[4,2,256,256]{3,2,1,0:T(8,128)(2,1)} %fusion.2), calls=%async_computation.6 | async-start | bytes 2097152 | tf_op jit(solution)/shard_map/all_to_all | solution.py:946
  463.7 21.8 %all-to-all-start.9 = ((bf16[8,304,256]{2,1,0:T(8,128)(2,1)}), bf16[8,304,256]{2,1,0:T(8,128)(2,1)}, u32[]{:S(2)}, u32[]{:S(2)}) async-start(bf16[8,304,256]{2,1,0:T(8,128)(2,1)} %broadcast_in_dim.86), calls=%async_computation.9 | async-start | bytes 2490368 | tf_op jit(solution)/shard_map/all_to_all | solution.py:946
  487.1 31.2 %all-to-all-start.7 = ((bf16[8,2,256,256]{3,2,1,0:T(8,128)(2,1)}), bf16[8,2,256,256]{3,2,1,0:T(8,128)(2,1)}, u32[]{:S(2)}, u32[]{:S(2)}) async-start(bf16[8,2,256,256]{3,2,1,0:T(8,128)(2,1)} %broadcast_in_dim.85), calls=%async_computation.7 | async-start | bytes 4194304 | tf_op jit(solution)/shard_map/all_to_all | solution.py:946
  491.7 7.3 %copy-start.5 = (bf16[1,512,1024]{1,2,0:T(8,128)(2,1)S(1)}, bf16[1,512,1024]{1,2,0:T(8,128)(2,1)}, u32[]{:S(2)}) copy-start(bf16[1,512,1024]{1,2,0:T(8,128)(2,1)} %copy-done.4) | copy-start | bytes 3145732
  (13 other events, 18.3 us)
